TPU v7x, 32 devices: a whole 2x2x4 slice. The times are simulated.
32 devices in a mesh: fsdp: 4 (over y, x), seq: 8 (over z, core).
Axes of the slice: x: 2, y: 2, z: 4, core: 2. Of those that a mesh axis runs over, the one named last changes fastest.
Arguments:
- images: bfloat16 [4, 1024, 1024], P('fsdp', 'seq'), may hold values from -7 to 7
- valid_mask: int32 [4, 1024], P('fsdp'), may hold values from 0 to 1, as said below
- ln1_gain: bfloat16 [1, 1024], P(None, ('fsdp', 'seq')), may hold values from 0.25 to 1.75
- ln1_bias: bfloat16 [1, 1024], P(None, ('fsdp', 'seq')), may hold values from -4 to 4
- qkv_weight: bfloat16 [1, 1024, 3072], P(None, ('fsdp', 'seq')), may hold values from -4 to 4
- q_bias: bfloat16 [1, 1024], P(None, ('fsdp', 'seq')), may hold values from -6 to 6
- v_bias: bfloat16 [1, 1024], P(None, ('fsdp', 'seq')), may hold values from -0.75 to 0.75
- proj_weight: bfloat16 [1, 1024, 1024], P(None, None, ('fsdp', 'seq')), may hold values from -12 to 12
- proj_bias: bfloat16 [1, 1024], P(None, ('fsdp', 'seq')), may hold values from -4 to 4
- ln2_gain: bfloat16 [1, 1024], P(None, ('fsdp', 'seq')), may hold values from 0.25 to 1.75
- ln2_bias: bfloat16 [1, 1024], P(None, ('fsdp', 'seq')), may hold values from -4 to 4
- fc1_weight: bfloat16 [1, 1024, 4096], P(None, ('fsdp', 'seq')), may hold values from -0.1875 to 0.1875
- fc1_bias: bfloat16 [1, 4096], P(None, ('fsdp', 'seq')), may hold values from -4 to 4
- fc2_weight: bfloat16 [1, 4096, 1024], P(None, None, ('fsdp', 'seq')), may hold values from -0.09375 to 0.09375
- fc2_bias: bfloat16 [1, 1024], P(None, ('fsdp', 'seq')), may hold values from -4 to 4
- out_grad: float32 [4, 1024, 1024], P('fsdp', 'seq'), may hold values from -6 to 6
Outputs:
- block_out: bfloat16 [4, 1024, 1024], P('fsdp', 'seq')
- images_grad: float32 [4, 1024, 1024], P('fsdp', 'seq')
- ln1_gain_grad: float32 [1, 1024], P(None, ('fsdp', 'seq'))
- ln1_bias_grad: float32 [1, 1024], P(None, ('fsdp', 'seq'))
- qkv_weight_grad: float32 [1, 1024, 3072], P(None, ('fsdp', 'seq'))
- q_bias_grad: float32 [1, 1024], P(None, ('fsdp', 'seq'))
- v_bias_grad: float32 [1, 1024], P(None, ('fsdp', 'seq'))
- proj_weight_grad: float32 [1, 1024, 1024], P(None, None, ('fsdp', 'seq'))
- proj_bias_grad: float32 [1, 1024], P(None, ('fsdp', 'seq'))
- ln2_gain_grad: float32 [1, 1024], P(None, ('fsdp', 'seq'))
- ln2_bias_grad: float32 [1, 1024], P(None, ('fsdp', 'seq'))
- fc1_weight_grad: float32 [1, 1024, 4096], P(None, ('fsdp', 'seq'))
- fc1_bias_grad: float32 [1, 4096], P(None, ('fsdp', 'seq'))
- fc2_weight_grad: float32 [1, 4096, 1024], P(None, None, ('fsdp', 'seq'))
- fc2_bias_grad: float32 [1, 1024], P(None, ('fsdp', 'seq'))
Inputs may be any that keep to these rules, and one draw needn't show every extreme that they name: valid_mask is 1 on the first tokens of each image and 0 on the rest; at least one and at most 256 of an image's last tokens are 0.
All inputs are finite; a program needn't handle non-finite values.
Results may differ from a plain program's by a relative error of at most 0.012.
Values may be sent and summed in bfloat16 or wider, within the bound.
No kernel may reach another device: no remote copies, remote signals or barrier semaphores. Data moves between devices by JAX's collectives and lax.ppermute only.
A program may use at most 192 MiB of HBM per device.

v0:
```python
import jax
import jax.numpy as jnp
from jax import lax
from jax.experimental import pallas as pl
from jax.experimental.pallas import tpu as pltpu
from jax.sharding import Mesh
from jax.sharding import PartitionSpec as P


HD = 64

epsilon = 1e-06
masked_score = -1e30
root_half = 0.7071067811865476
inv_root_tau = 0.3989422804014327
f32 = jnp.float32
bf16 = jnp.bfloat16
ALL = ("fsdp", "z", "core")
SEQ = ("z", "core")


def normalize(hidden):
    center = hidden - jnp.mean(hidden, axis=-1, keepdims=True)
    spread = lax.rsqrt(jnp.mean(center * center, axis=-1, keepdims=True) + epsilon)
    return (center * spread, spread)


def norm_back(grad_in, normed, spread, gain_vec):
    scaled = grad_in * gain_vec
    return spread * (
        scaled
        - jnp.mean(scaled, axis=-1, keepdims=True)
        - normed * jnp.mean(scaled * normed, axis=-1, keepdims=True)
    )


def mm(a, b, ca=1, cb=0):
    return lax.dot_general(a, b, (((ca,), (cb,)), ((), ())), preferred_element_type=f32)


def lanes_of(block, head):
    lane = lax.broadcasted_iota(jnp.int32, block.shape, 1)
    return jnp.where(lane // HD == head, block, jnp.zeros_like(block))


def attn_fwd_body(one_ref, two_ref, ok_ref, out_ref, log_ref, all_ref):
    half = one_ref.shape[0]
    qb, width = out_ref.shape
    heads = width // HD
    step = pl.program_id(0)

    @pl.when(step == 0)
    def _():
        all_ref[:half] = one_ref[...]
        all_ref[half:] = two_ref[...]

    queries = all_ref[pl.ds(step * qb, qb), :width] * 0.125
    keys = all_ref[:, width : 2 * width]
    values = all_ref[:, 2 * width :]
    valid = ok_ref[...] > 0
    tops = []
    logs = []
    for head in range(heads):
        scores = mm(keys, lanes_of(queries, head), 1, 1)
        scores = jnp.where(valid, scores, masked_score)
        top = jnp.max(scores, axis=0, keepdims=True)
        powers = jnp.exp(scores - top)
        total = jnp.sum(powers, axis=0, keepdims=True)
        probs = (powers * (1.0 / total)).astype(bf16)
        mixed = mm(values, probs, 0, 0)
        tops.append(mixed[head * HD : (head + 1) * HD])
        logs.append(top + jnp.log(total))
    out_ref[...] = jnp.concatenate(tops, axis=0).T.astype(bf16)
    log_ref[...] = jnp.concatenate(logs, axis=0)


def attn_bwd_body(
    g_ref, log_ref, one_ref, two_ref, ok_ref, out_ref, sum_ref, all_ref, dk_acc, dv_acc
):
    half = one_ref.shape[0]
    qb, width = g_ref.shape
    heads = width // HD
    step = pl.program_id(0)

    @pl.when(step == 0)
    def _():
        all_ref[:half] = one_ref[...]
        all_ref[half:] = two_ref[...]
        dk_acc[...] = jnp.zeros_like(dk_acc)
        dv_acc[...] = jnp.zeros_like(dv_acc)

    queries = all_ref[pl.ds(step * qb, qb), :width] * 0.125
    keys = all_ref[:, width : 2 * width]
    values = all_ref[:, 2 * width :]
    grads = g_ref[...]
    valid = ok_ref[...] > 0
    logs = log_ref[...]
    parts = []
    key_sum = dk_acc[...]
    value_sum = dv_acc[...]
    for head in range(heads):
        q_head = lanes_of(queries, head)
        g_head = lanes_of(grads, head)
        scores = mm(keys, q_head, 1, 1)
        scores = jnp.where(valid, scores, masked_score)
        weights = jnp.exp(scores - logs[head : head + 1])
        prob_grad = mm(values, g_head, 1, 1)
        delta = jnp.sum(weights * prob_grad, axis=0, keepdims=True)
        score_grad = (weights * (prob_grad - delta)).astype(bf16)
        value_sum = value_sum + mm(weights.astype(bf16), g_head)
        key_sum = key_sum + mm(score_grad, q_head)
        mixed = mm(keys, score_grad, 0, 0)
        parts.append(mixed[head * HD : (head + 1) * HD])
    dk_acc[...] = key_sum
    dv_acc[...] = value_sum
    dq = (0.125 * jnp.concatenate(parts, axis=0).T).astype(bf16)
    out_ref[pl.ds(step * qb, qb), :width] = dq

    @pl.when(step == pl.num_programs(0) - 1)
    def _():
        out_ref[:, width : 2 * width] = dk_acc[...].astype(bf16)
        out_ref[:, 2 * width :] = dv_acc[...].astype(bf16)
        sum_ref[...] = jnp.sum(out_ref[...].astype(f32), axis=0, keepdims=True)


def attn_fwd(one, two, valid_col):
    n, w = valid_col.shape[0], one.shape[1] // 3
    heads = w // HD
    qb = min(256, n)
    whole = lambda i: (0, 0)
    return pl.pallas_call(
        attn_fwd_body,
        grid=(n // qb,),
        in_specs=[
            pl.BlockSpec((n // 2, 3 * w), whole),
            pl.BlockSpec((n // 2, 3 * w), whole),
            pl.BlockSpec((n, 1), whole),
        ],
        out_specs=[
            pl.BlockSpec((qb, w), lambda i: (i, 0)),
            pl.BlockSpec((heads, qb), lambda i: (0, i)),
        ],
        out_shape=[
            jax.ShapeDtypeStruct((n, w), bf16),
            jax.ShapeDtypeStruct((heads, n), f32),
        ],
        scratch_shapes=[pltpu.VMEM((n, 3 * w), bf16)],
        name="attn_fwd",
    )(one, two, valid_col)


def attn_bwd(grad, logs, one, two, valid_col):
    n, w = grad.shape
    heads = w // HD
    qb = min(256, n)
    whole = lambda i: (0, 0)
    return pl.pallas_call(
        attn_bwd_body,
        grid=(n // qb,),
        in_specs=[
            pl.BlockSpec((qb, w), lambda i: (i, 0)),
            pl.BlockSpec((heads, qb), lambda i: (0, i)),
            pl.BlockSpec((n // 2, 3 * w), whole),
            pl.BlockSpec((n // 2, 3 * w), whole),
            pl.BlockSpec((n, 1), whole),
        ],
        out_specs=[pl.BlockSpec((n, 3 * w), whole), pl.BlockSpec((1, 3 * w), whole)],
        out_shape=[
            jax.ShapeDtypeStruct((n, 3 * w), bf16),
            jax.ShapeDtypeStruct((1, 3 * w), f32),
        ],
        scratch_shapes=[
            pltpu.VMEM((n, 3 * w), bf16),
            pltpu.VMEM((n, w), f32),
            pltpu.VMEM((n, w), f32),
        ],
        name="attn_bwd",
    )(grad, logs, one, two, valid_col)


def ffn_grads_body(m0, m1, p0, p1, g0, g1, a0, a1, out_ref):
    blocks, _, rows, width = out_ref.shape
    hidden = width // 2
    up = mm(m0[...], p0[...], 0, 0) + mm(m1[...], p1[...], 0, 0)
    down = mm(g0[...], a0[...], 0, 0) + mm(g1[...], a1[...], 0, 0)
    for z in range(blocks):
        out_ref[z, 0, :, :hidden] = up[z * rows : (z + 1) * rows].astype(bf16)
        out_ref[z, 0, :, hidden:] = down[z * rows : (z + 1) * rows].astype(bf16)


def ffn_grads(mlp_halves, pre_low, grad_halves, activated, F, Z):
    tokens, D = mlp_halves[0].shape
    B = pre_low[0].shape[1]
    cols = pl.BlockSpec((tokens, D // F), lambda f: (0, f))
    whole = pl.BlockSpec((tokens, B), lambda f: (0, 0))
    rows = D // (F * Z)
    return pl.pallas_call(
        ffn_grads_body,
        grid=(F,),
        in_specs=[cols, cols, whole, whole] * 2,
        out_specs=pl.BlockSpec((Z, 1, rows, 2 * B), lambda f: (0, f, 0, 0)),
        out_shape=jax.ShapeDtypeStruct((Z, F, rows, 2 * B), bf16),
        name="ffn_grads",
    )(*mlp_halves, *pre_low, *grad_halves, *activated)


def make_shards(F, Z):
    S = 2 * Z
    N_DEV = F * S
    PL = 2 * F

    def swap(x, kf=0, kz=0, kc=0):
        pairs = []
        for f in range(F):
            for z in range(Z):
                for c in range(2):
                    src = (f * Z + z) * 2 + c
                    pairs.append((src, ((f ^ kf) * Z + (z ^ kz)) * 2 + (c ^ kc)))
        return lax.ppermute(x, ALL, pairs)

    def reorder(x, index, axis=0):
        size = x.shape[axis]
        shape = x.shape
        for bit in range(size.bit_length() - 1):
            low = 1 << bit
            split = x.reshape(shape[:axis] + (size // (2 * low), 2, low) + shape[axis + 1 :])
            flipped = jnp.flip(split, axis=axis + 1)
            x = jnp.where((index >> bit) & 1 == 1, flipped, split).reshape(shape)
        return x

    def gather_halves(x, outer, axis_name):
        blocks = [x]
        for k in range(1, outer):
            blocks.append(swap(x, **{axis_name: k}))
        mine = jnp.concatenate(blocks, axis=0)
        return mine, swap(mine, kc=1)

    def scatter_sum(mine, other, outer, axis_name):
        other = swap(other.astype(bf16), kc=1)
        mine = lax.optimization_barrier(mine)
        half = (mine + other.astype(f32)).astype(bf16)
        half = half.reshape(outer, -1, half.shape[-1])
        total = half[0].astype(f32)
        for k in range(1, outer):
            part = swap(half[k], **{axis_name: k})
            total = total + part.astype(f32)
        return total

    def place(block, count, axis_name, index, axis):
        shape = block.shape[:axis] + (count,) + block.shape[axis:]
        out = jnp.zeros(shape, block.dtype)
        for k in range(count):
            part = block if k == 0 else swap(block, **{axis_name: k})
            out = lax.dynamic_update_slice_in_dim(
                out, jnp.expand_dims(part, axis), index ^ k, axis
            )
        return out

    def reduce_over(x, count, axis_name, index, axis):
        total = lax.dynamic_index_in_dim(x, index, axis, keepdims=False).astype(f32)
        for k in range(1, count):
            part = lax.dynamic_index_in_dim(x, index ^ k, axis, keepdims=False)
            part = swap(part, **{axis_name: k})
            total = total + part.astype(f32)
        return total

    def exchange(x, axes):
        return lax.all_to_all(x, axes, split_axis=0, concat_axis=0, tiled=True)

    def shards(
        images,
        valid_mask,
        ln1_gain,
        ln1_bias,
        qkv_weight,
        q_bias,
        v_bias,
        proj_weight,
        proj_bias,
        ln2_gain,
        ln2_bias,
        fc1_weight,
        fc1_bias,
        fc2_weight,
        fc2_bias,
        out_grad,
    ):
        _, T, D = images.shape
        R = D // N_DEV
        FF = fc1_weight.shape[2]
        W = D // S
        B = FF // PL
        Q = FF // D
        N = S * T
        fi = lax.axis_index("fsdp")
        zi = lax.axis_index("z")
        ci = lax.axis_index("core")
        si = zi * 2 + ci
        pi = fi * 2 + ci

        x_own = images[0]
        grad_own = out_grad[0]
        x_halves = gather_halves(x_own, Z, "kz")

        vecs = [ln1_gain, ln1_bias, q_bias, v_bias, proj_bias, ln2_gain, ln2_bias, fc2_bias]
        count = len(vecs) + Q
        side = jnp.concatenate(vecs + [fc1_bias.reshape(Q, R)], axis=0)
        side = jnp.pad(side, ((0, -count % 16), (0, 3 * W - R)))
        w_qkv = qkv_weight[0].reshape(R, 3, S, W).transpose(2, 0, 1, 3).reshape(S, R, 3 * W)
        w_qkv = jnp.concatenate(
            [w_qkv, jnp.broadcast_to(side[None], (S,) + side.shape)], axis=1
        )
        w_qkv = exchange(w_qkv, SEQ)
        w_qkv = place(w_qkv, F, "kf", fi, 0)
        side = w_qkv[:, :, R : R + count, :R].astype(f32).reshape(N_DEV, count, R)
        w_qkv = w_qkv[:, :, :R].reshape(D, 3 * W)
        side_t = side[:, : len(vecs)].transpose(1, 0, 2).reshape(len(vecs), D)
        gain_one, shift_one, bias_q, bias_v, proj_shift, gain_two, shift_two, down_shift = [
            side_t[i : i + 1] for i in range(len(vecs))
        ]
        up_shift = lax.dynamic_slice_in_dim(side, pi * Z, Z, 0)[:, len(vecs) :].reshape(1, B)

        block = place(proj_weight[0].T, Z, "kz", zi, 0)
        block = place(block, F, "kf", fi, 0)
        proj_t = place(block, 2, "kc", ci, 2).reshape(D, D)

        w_ffn = jnp.concatenate(
            [fc1_weight[0].reshape(R, PL, B), fc2_weight[0].T.reshape(R, PL, B)], axis=2
        ).transpose(1, 0, 2)
        w_ffn = exchange(w_ffn, ("fsdp", "core")).reshape(F, 2, R, 2 * B)
        w_ffn = place(w_ffn, Z, "kz", zi, 1).reshape(D, 2 * B)
        w_up = w_ffn[:, :B]
        w_down_t = w_ffn[:, B:]

        grad_halves = gather_halves(grad_own.astype(bf16), F, "kf")

        valid_col = valid_mask[0].reshape(Z, 2, T).transpose(1, 0, 2)
        valid_col = reorder(reorder(valid_col, ci, 0), zi, 1).reshape(N, 1)
        my_cols = lambda vec: lax.dynamic_slice(vec, (0, si * W), (1, W))
        bias_row = jnp.concatenate([my_cols(bias_q), jnp.zeros((1, W), f32), my_cols(bias_v)], axis=1)
        normed_all, attn_in, qkv = [], [], []
        for part in x_halves:
            normed, _ = normalize(part.astype(f32))
            normed_all.append(normed)
            attn_in.append((normed * gain_one + shift_one).astype(bf16))
            qkv.append((mm(attn_in[-1], w_qkv) + bias_row).astype(bf16))
        mixed, logs = attn_fwd(qkv[0], qkv[1], valid_col)
        mixed = reorder(reorder(mixed.reshape(2, Z, T, W), ci, 0), zi, 1)
        mixed = mixed.transpose(1, 0, 2, 3).reshape(S, T, W)
        attended = exchange(mixed, SEQ)
        attended = attended.transpose(1, 0, 2).reshape(T, D)

        hidden = x_own.astype(f32)
        after_attn = hidden + mm(attended, proj_t, 1, 1) + proj_shift
        normed_two, spread_two = normalize(after_attn)
        mlp_in = (normed_two * gain_two + shift_two).astype(bf16)

        mlp_halves = gather_halves(mlp_in, F, "kf")
        activated, pre_low = [], []
        up_shift_grad = 0.0
        for mlp_part, grad_part in zip(mlp_halves, grad_halves):
            pre_act = mm(mlp_part, w_up) + up_shift
            erf_part = lax.erf(pre_act * root_half)
            activated.append((0.5 * pre_act * (1.0 + erf_part)).astype(bf16))
            slope = 0.5 * (1.0 + erf_part) + pre_act * inv_root_tau * jnp.exp(
                -0.5 * pre_act * pre_act
            )
            pre_grad = mm(grad_part, w_down_t) * slope
            pre_low.append(pre_grad.astype(bf16))
            up_shift_grad = up_shift_grad + jnp.sum(pre_grad, axis=0)
        mlp_part = mm(pre_low[0], w_up, 1, 1)
        mlp_grad = scatter_sum(mlp_part, mm(pre_low[1], w_up, 1, 1), F, "kf")

        ffn_grad = ffn_grads(mlp_halves, pre_low, grad_halves, activated, F, Z)
        ffn_grad = reduce_over(ffn_grad, Z, "kz", zi, 0)
        ffn_grad = exchange(ffn_grad.astype(bf16).reshape(PL, R, 2 * B), ("fsdp", "core"))
        ffn_grad = ffn_grad.astype(f32)
        up_grad = ffn_grad[..., :B].transpose(1, 0, 2).reshape(1, R, FF)
        down_grad = ffn_grad[..., B:].transpose(0, 2, 1).reshape(1, FF, R)
        mid_grad = grad_own + norm_back(mlp_grad, normed_two, spread_two, gain_two)
        mid_low = mid_grad.astype(bf16)
        mid_low, after_late, activated[0], activated[1] = lax.optimization_barrier(
            (mid_low, after_attn, activated[0], activated[1])
        )
        down_out = scatter_sum(
            mm(activated[0], w_down_t, 1, 1), mm(activated[1], w_down_t, 1, 1), F, "kf"
        )
        block_out = (after_late + down_out + down_shift).astype(bf16)

        attended_grad = mm(mid_low, proj_t, 1, 0).astype(bf16)
        attended_grad = exchange(attended_grad.reshape(T, S, W).transpose(1, 0, 2), SEQ)
        attended_grad = attended_grad.reshape(Z, 2, T, W).transpose(1, 0, 2, 3)
        attended_grad = reorder(reorder(attended_grad, ci, 0), zi, 1).reshape(N, W)

        proj_grad = mm(mid_low, attended, 0, 0).astype(bf16)
        proj_grad = reduce_over(proj_grad.reshape(F, Z, 2, R, D), 2, "kc", ci, 2)
        proj_grad = reduce_over(proj_grad.astype(bf16), F, "kf", fi, 0)
        proj_grad = reduce_over(proj_grad.astype(bf16), Z, "kz", zi, 0)
        proj_grad = proj_grad.T.reshape(1, D, R)

        qkv_grad, qkv_sums = attn_bwd(attended_grad, logs, qkv[0], qkv[1], valid_col)
        qkv_halves = (qkv_grad[: N // 2], qkv_grad[N // 2 :])
        in_late = mm(qkv_halves[1], w_qkv, 1, 1)
        late_low, first = lax.optimization_barrier((in_late.astype(bf16), qkv_halves[0]))
        in_grads = [mm(first, w_qkv, 1, 1), in_late]
        gain_one_grad = sum(jnp.sum(a * b, axis=0) for a, b in zip(in_grads, normed_all))
        shift_one_grad = sum(jnp.sum(a, axis=0) for a in in_grads)
        attn_in_grad = scatter_sum(in_grads[0], late_low, Z, "kz")
        normed_one, spread_one = normalize(hidden)
        images_grad = mid_grad + norm_back(attn_in_grad, normed_one, spread_one, gain_one)

        w_grad = sum(mm(a, g, 0, 0) for a, g in zip(attn_in, qkv_halves)).astype(bf16)
        w_grad = reduce_over(w_grad.reshape(F, S, R, 3 * W), F, "kf", fi, 0)
        w_grad = exchange(w_grad.astype(bf16), SEQ).astype(f32)
        qkv_weight_grad = jnp.concatenate(
            [
                w_grad[..., i * W : (i + 1) * W].transpose(1, 0, 2).reshape(1, R, D)
                for i in range(3)
            ],
            axis=2,
        )

        my_slots = lambda part: lax.dynamic_update_slice(jnp.zeros((D,), f32), part, (si * W,))
        parts = [
            gain_one_grad,
            shift_one_grad,
            my_slots(qkv_sums[0, :W]),
            my_slots(qkv_sums[0, 2 * W :]),
            jnp.sum(mid_grad, axis=0),
            jnp.sum(mlp_grad * normed_two, axis=0),
            jnp.sum(mlp_grad, axis=0),
            jnp.sum(grad_own, axis=0),
            lax.dynamic_update_slice(jnp.zeros((FF,), f32), up_shift_grad, (pi * B,)),
        ]
        sums = jnp.concatenate([part.reshape(N_DEV, -1) for part in parts], axis=1)
        sums = exchange(sums.reshape(N_DEV, 1, -1), ALL)
        sums = jnp.sum(sums, axis=0)
        g = [sums[:, i * R : (i + 1) * R] for i in range(8)]
        return (
            block_out[None],
            images_grad[None],
            g[0],
            g[1],
            qkv_weight_grad,
            g[2],
            g[3],
            proj_grad,
            g[4],
            g[5],
            g[6],
            up_grad,
            sums[:, 8 * R :],
            down_grad,
            g[7],
        )

    return shards


def solution(mesh):
    F, S = mesh.shape["fsdp"], mesh.shape["seq"]
    Z = S // 2
    split = Mesh(mesh.devices.reshape(F, Z, 2), ALL)
    tok = P("fsdp", SEQ, None)
    vec = P(None, ALL)
    rows = P(None, ALL, None)
    cols = P(None, None, ALL)
    in_specs = (
        tok, P("fsdp", None), vec, vec, rows, vec, vec, cols, vec, vec, vec, rows, vec, cols, vec, tok,
    )
    out_specs = (tok, tok, vec, vec, rows, vec, vec, cols, vec, vec, vec, rows, vec, cols, vec)
    inner = make_shards(F, Z)

    return jax.shard_map(inner, mesh=split, in_specs=in_specs, out_specs=out_specs, check_vma=False)
```

profile of v0, /device:TPU:0, one launch (start us, length us, event | category | flops | bytes accessed | tf_op | source)
XLA Modules:
  0.0 386.0 jit_solution(6278067999464942186)
XLA Ops:
  0.7 3.1 collective-permute-start.7
  3.8 2.6 collective-permute-start.8
  7.3 3.5 collective-permute-start.1
  15.5 3.6 all-to-all-start
  22.9 3.7 collective-permute-start.2
  38.7 3.6 collective-permute-done.15
  44.8 2.6 collective-permute-done.10
  48.1 5.0 %collective-permute-done.11 = bf16[4,32,1024]{2,1,0:T(8,128)(2,1)S(1)} collective-permute-done((bf16[4,32,1024]{2,1,0:T(8,128)(2,1)S(1)}, bf16[4,32,1024]{2,1,0:T(8,128)(2,1)S(1)}, u32[]{:S(2)}, u32[]{:S(2)}) %collective-permute-start.11) | collective-permute-done | bytes 262176 | tf_op jit(solution)/shard_map/ppermute | solution.py:219
  53.9 4.2 %all-to-all-start.2 = ((bf16[8,32,1024]{2,1,0:T(8,128)(2,1)}), bf16[8,32,1024]{2,1,0:T(8,128)(2,1)}, u32[]{:S(2)}, u32[]{:S(2)}) async-start(bf16[8,32,1024]{2,1,0:T(8,128)(2,1)} %maximum_bitcast_fusion), calls=%async_computation.2 | async-start | bytes 1048576 | tf_op jit(solution)/shard_map/all_to_all | solution.py:268
  63.5 10.1 %collective-permute-done.3 = bf16[8,48,384]{2,1,0:T(8,128)(2,1)S(1)} collective-permute-done((bf16[8,48,384]{2,1,0:T(8,128)(2,1)S(1)}, bf16[8,48,384]{2,1,0:T(8,128)(2,1)S(1)}, u32[]{:S(2)}, u32[]{:S(2)}) %collective-permute-start.3) | collective-permute-done | bytes 294944 | tf_op jit(solution)/shard_map/ppermute | solution.py:219
  73.7 6.6 %collective-permute-done.5 = bf16[8,48,384]{2,1,0:T(8,128)(2,1)S(1)} collective-permute-done((bf16[8,48,384]{2,1,0:T(8,128)(2,1)S(1)}, bf16[8,48,384]{2,1,0:T(8,128)(2,1)S(1)}, u32[]{:S(2)}, u32[]{:S(2)}) %collective-permute-start.5) | collective-permute-done | bytes 294944 | tf_op jit(solution)/shard_map/ppermute | solution.py:219
  85.7 9.5 %attn_fwd.1 = (bf16[1024,128]{1,0:T(8,128)(2,1)}, f32[2,1024]{1,0:T(2,128)}) custom-call(bf16[512,384]{1,0:T(8,128)(2,1)} %fusion.17.one_ref, bf16[512,384]{1,0:T(8,128)(2,1)} %fusion.18.two_ref, s32[1024,1]{1,0:T(8,128)} %copy.60.ok_ref), custom_call_target="tpu_custom_call" | custom-call | tf_op jit(solution)/shard_map/attn_fwd/pallas_call | solution.py:131
  97.2 4.1 %all-to-all-start.1 = ((bf16[8,128,128]{2,1,0:T(8,128)(2,1)}), bf16[8,128,128]{2,1,0:T(8,128)(2,1)S(1)}, u32[]{:S(2)}, u32[]{:S(2)}) async-start(bf16[8,128,128]{2,1,0:T(8,128)(2,1)} %bitcast.20), calls=%async_computation.1 | async-start | bytes 524288 | tf_op jit(solution)/shard_map/all_to_all | solution.py:268
  105.0 2.4 collective-permute-start.18
  114.9 2.6 collective-permute-start.22
  118.3 12.6 %collective-permute-done.17 = bf16[4,2,32,1024]{3,2,1,0:T(8,128)(2,1)} collective-permute-done((bf16[4,2,32,1024]{3,2,1,0:T(8,128)(2,1)}, bf16[4,2,32,1024]{3,2,1,0:T(8,128)(2,1)}, u32[]{:S(2)}, u32[]{:S(2)}) %collective-permute-start.17) | collective-permute-done | bytes 524320 | tf_op jit(solution)/shard_map/ppermute | solution.py:219
  137.9 8.6 %collective-permute-done.19 = bf16[4,2,32,1024]{3,2,1,0:T(8,128)(2,1)S(1)} collective-permute-done((bf16[4,2,32,1024]{3,2,1,0:T(8,128)(2,1)}, bf16[4,2,32,1024]{3,2,1,0:T(8,128)(2,1)S(1)}, u32[]{:S(2)}, u32[]{:S(2)}) %collective-permute-start.19) | collective-permute-done | bytes 524320 | tf_op jit(solution)/shard_map/ppermute | solution.py:219
  147.3 3.1 multiply_convert_fusion.1
  150.5 3.1 fusion.78
  153.6 3.2 multiply_convert_fusion
  156.8 3.4 fusion.77
  160.2 6.5 %ffn_grads.1 = bf16[4,4,64,1024]{3,2,1,0:T(8,128)(2,1)} custom-call(bf16[512,1024]{1,0:T(8,128)(2,1)} %copy-done.7, bf16[512,1024]{1,0:T(8,128)(2,1)} %copy-done.14, bf16[512,512]{1,0:T(8,128)(2,1)} %get-tuple-element.71.p0, bf16[512,512]{1,0:T(8,128)(2,1)} %get-tuple-element.69.p1, bf16[512,1024]{1,0:T(8,128)(2,1)} %pad_maximum_fusion.1.g0, ...), custom_call_target="tpu_custom_call" | custom-call | tf_op jit(solution)/shard_map/ffn_grads/pallas_call | solution.py:197
  166.7 2.6 dynamic-slice_bitcast_fusion.3
  169.3 10.1 %collective-permute-start.47 = (bf16[4,64,1024]{2,1,0:T(8,128)(2,1)}, bf16[4,64,1024]{2,1,0:T(8,128)(2,1)}, u32[]{:S(2)}, u32[]{:S(2)}) collective-permute-start(bf16[4,64,1024]{2,1,0:T(8,128)(2,1)} %get-tuple-element.59), channel_id=1, source_target_pairs={{0,2},{1,3},{2,0},{3,1},{4,6},{5,7},{6,4},{7,5},{8,10},{9,11},{10,... | collective-permute-start | bytes 1572872 | tf_op jit(solution)/shard_map/ppermute | solution.py:219
  179.4 2.4 collective-permute-start.49
  181.8 2.9 convolution_convert_fusion.2
  186.2 15.2 %collective-permute-done.47 = bf16[4,64,1024]{2,1,0:T(8,128)(2,1)} collective-permute-done((bf16[4,64,1024]{2,1,0:T(8,128)(2,1)}, bf16[4,64,1024]{2,1,0:T(8,128)(2,1)}, u32[]{:S(2)}, u32[]{:S(2)}) %collective-permute-start.47) | collective-permute-done | bytes 524320 | tf_op jit(solution)/shard_map/ppermute | solution.py:219
  201.4 16.4 %collective-permute-done.48 = bf16[4,64,1024]{2,1,0:T(8,128)(2,1)} collective-permute-done((bf16[4,64,1024]{2,1,0:T(8,128)(2,1)}, bf16[4,64,1024]{2,1,0:T(8,128)(2,1)}, u32[]{:S(2)}, u32[]{:S(2)}) %collective-permute-start.48) | collective-permute-done | bytes 524320 | tf_op jit(solution)/shard_map/ppermute | solution.py:219
  217.9 2.7 fusion.29
  220.5 4.2 %all-to-all-start.6 = ((bf16[8,32,1024]{2,1,0:T(8,128)(2,1)}), bf16[8,32,1024]{2,1,0:T(8,128)(2,1)}, u32[]{:S(2)}, u32[]{:S(2)}) async-start(bf16[8,32,1024]{2,1,0:T(8,128)(2,1)} %bitcast.219), calls=%async_computation.6 | async-start | bytes 1048576 | tf_op jit(solution)/shard_map/all_to_all | solution.py:268
  224.7 3.3 fusion.32
  228.1 6.3 %all-to-all-done.6 = bf16[8,32,1024]{2,1,0:T(8,128)(2,1)} async-done(((bf16[8,32,1024]{2,1,0:T(8,128)(2,1)}), bf16[8,32,1024]{2,1,0:T(8,128)(2,1)}, u32[]{:S(2)}, u32[]{:S(2)}) %all-to-all-start.6) | async-done | bytes 524320 | tf_op jit(solution)/shard_map/all_to_all | solution.py:268
  239.9 2.4 collective-permute-start.28
  248.3 5.0 %collective-permute-done.27 = bf16[128,1024]{1,0:T(8,128)(2,1)} collective-permute-done((bf16[128,1024]{1,0:T(8,128)(2,1)}, bf16[128,1024]{1,0:T(8,128)(2,1)}, u32[]{:S(2)}, u32[]{:S(2)}) %collective-permute-start.27) | collective-permute-done | bytes 262176 | tf_op jit(solution)/shard_map/ppermute | solution.py:219
  257.6 11.6 %all-to-all-start.3 = ((bf16[8,128,128]{2,1,0:T(8,128)(2,1)}), bf16[8,128,128]{2,1,0:T(8,128)(2,1)}, u32[]{:S(2)}, u32[]{:S(2)}) async-start(bf16[8,128,128]{2,1,0:T(8,128)(2,1)} %bitcast.203), calls=%async_computation.3 | async-start | bytes 524288 | tf_op jit(solution)/shard_map/all_to_all | solution.py:268
  272.9 3.1 convolution_convert_fusion.1
  276.0 3.1 all-to-all-done.3
  281.0 10.5 %attn_bwd.1 = (bf16[1024,384]{1,0:T(8,128)(2,1)}, f32[1,384]{1,0:T(1,128)}) custom-call(bf16[1024,128]{1,0:T(8,128)(2,1)} %bitcast.225, f32[2,1024]{1,0:T(2,128)} %get-tuple-element.30.log_ref, bf16[512,384]{1,0:T(8,128)(2,1)} %fusion.17.one_ref, bf16[512,384]{1,0:T(8,128)(2,1)} %fusion.18.two_ref, s32[1024,1]{1,0:T(8,128)} %copy.60.ok_ref), custom_call_target="tpu_custom_call" | custom-call | tf_op jit(solution)/shard_map/attn_bwd/pallas_call | solution.py:157
  292.6 2.3 fusion.56
  308.3 2.6 all-to-all-start.4
  312.9 5.3 %all-to-all-done.4 = f32[32,1,384]{2,1,0:T(1,128)S(1)} async-done(((f32[32,1,384]{2,1,0:T(1,128)}), f32[32,1,384]{2,1,0:T(1,128)S(1)}, u32[]{:S(2)}, u32[]{:S(2)}) %all-to-all-start.4) | async-done | bytes 49184 | tf_op jit(solution)/shard_map/all_to_all | solution.py:268
  318.2 4.3 %all-to-all-start.5 = ((bf16[8,32,384]{2,1,0:T(8,128)(2,1)}), bf16[8,32,384]{2,1,0:T(8,128)(2,1)}, u32[]{:S(2)}, u32[]{:S(2)}) async-start(bf16[8,32,384]{2,1,0:T(8,128)(2,1)} %fusion.55), calls=%async_computation.5 | async-start | bytes 393216 | tf_op jit(solution)/shard_map/all_to_all | solution.py:268
  322.5 3.5 fusion.36
  327.2 3.3 all-to-all-done.5
  346.0 3.3 collective-permute-done.41
  349.9 3.5 collective-permute-done.42
  370.2 5.3 %collective-permute-done.34 = bf16[128,1024]{1,0:T(8,128)(2,1)S(1)} collective-permute-done((bf16[128,1024]{1,0:T(8,128)(2,1)S(1)}, bf16[128,1024]{1,0:T(8,128)(2,1)S(1)}, u32[]{:S(2)}, u32[]{:S(2)}) %collective-permute-start.34) | collective-permute-done | bytes 262176 | tf_op jit(solution)/shard_map/ppermute | solution.py:219
  375.5 9.1 %collective-permute-done.35 = bf16[128,1024]{1,0:T(8,128)(2,1)S(1)} collective-permute-done((bf16[128,1024]{1,0:T(8,128)(2,1)S(1)}, bf16[128,1024]{1,0:T(8,128)(2,1)S(1)}, u32[]{:S(2)}, u32[]{:S(2)}) %collective-permute-start.35) | collective-permute-done | bytes 262176 | tf_op jit(solution)/shard_map/ppermute | solution.py:219
  (328 shorter events, 132.6 us)
Async XLA Ops:
  0.7 22.2 %collective-permute-start.7 = (bf16[32,1024]{1,0:T(8,128)(2,1)}, bf16[32,1024]{1,0:T(8,128)(2,1)S(1)}, u32[]{:S(2)}, u32[]{:S(2)}) collective-permute-start(bf16[32,1024]{1,0:T(8,128)(2,1)} %bitcast.239), channel_id=1, source_target_pairs={{0,2},{1,3},{2,0},{3,1},{4,6},{5,7},{6,4},{7,5},{8,10},{9,11},{10,... | collective-permute-start | bytes 196616 | tf_op jit(solution)/shard_map/ppermute | solution.py:219
  3.8 22.8 %collective-permute-start.8 = (bf16[32,1024]{1,0:T(8,128)(2,1)}, bf16[32,1024]{1,0:T(8,128)(2,1)S(1)}, u32[]{:S(2)}, u32[]{:S(2)}) collective-permute-start(bf16[32,1024]{1,0:T(8,128)(2,1)} %bitcast.240), channel_id=1, source_target_pairs={{0,4},{1,5},{2,6},{3,7},{4,0},{5,1},{6,2},{7,3},{8,12},{9,13},{10,... | collective-permute-start | bytes 196616 | tf_op jit(solution)/shard_map/ppermute | solution.py:219
  6.4 21.8 %collective-permute-start.9 = (bf16[32,1024]{1,0:T(8,128)(2,1)}, bf16[32,1024]{1,0:T(8,128)(2,1)S(1)}, u32[]{:S(2)}, u32[]{:S(2)}) collective-permute-start(bf16[32,1024]{1,0:T(8,128)(2,1)} %bitcast.241), channel_id=1, source_target_pairs={{0,6},{1,7},{2,4},{3,5},{4,2},{5,3},{6,0},{7,1},{8,14},{9,15},{10,... | collective-permute-start | bytes 196616 | tf_op jit(solution)/shard_map/ppermute | solution.py:219
  6.4 25.2 %collective-permute-start = (bf16[128,1024]{1,0:T(8,128)(2,1)}, bf16[128,1024]{1,0:T(8,128)(2,1)S(1)}, u32[]{:S(2)}, u32[]{:S(2)}) collective-permute-start(bf16[128,1024]{1,0:T(8,128)(2,1)} %bitcast.211), channel_id=1, source_target_pairs={{0,2},{1,3},{2,0},{3,1},{4,6},{5,7},{6,4},{7,5},{8,10},{9,11},{10,... | collective-permute-start | bytes 786440 | tf_op jit(solution)/shard_map/ppermute | solution.py:219
  7.3 24.8 %collective-permute-start.1 = (bf16[128,1024]{1,0:T(8,128)(2,1)}, bf16[128,1024]{1,0:T(8,128)(2,1)S(1)}, u32[]{:S(2)}, u32[]{:S(2)}) collective-permute-start(bf16[128,1024]{1,0:T(8,128)(2,1)} %bitcast.212), channel_id=1, source_target_pairs={{0,4},{1,5},{2,6},{3,7},{4,0},{5,1},{6,2},{7,3},{8,12},{9,13},{10,... | collective-permute-start | bytes 786440 | tf_op jit(solution)/shard_map/ppermute | solution.py:219
  15.5 38.3 %all-to-all-start = ((bf16[8,48,384]{2,1,0:T(8,128)(2,1)}), bf16[8,48,384]{2,1,0:T(8,128)(2,1)S(1)}, u32[]{:S(2)}, u32[]{:S(2)}) async-start(bf16[8,48,384]{2,1,0:T(8,128)(2,1)} %pad_maximum_fusion.4), calls=%async_computation | async-start | bytes 589824 | tf_op jit(solution)/shard_map/all_to_all | solution.py:268
  22.9 11.6 %collective-permute-start.2 = (bf16[128,1024]{1,0:T(8,128)(2,1)S(1)}, bf16[128,1024]{1,0:T(8,128)(2,1)S(1)}, u32[]{:S(2)}, u32[]{:S(2)}) collective-permute-start(bf16[128,1024]{1,0:T(8,128)(2,1)S(1)} %bitcast.213), channel_id=1, source_target_pairs={{0,6},{1,7},{2,4},{3,5},{4,2},{5,3},{6,0},{7,1},{8,14},{9,15},{10,... | collective-permute-start | bytes 786440 | tf_op jit(solution)/shard_map/ppermute | solution.py:219
  28.2 14.1 %collective-permute-start.15 = (bf16[128,1024]{1,0:T(8,128)(2,1)}, bf16[128,1024]{1,0:T(8,128)(2,1)S(1)}, u32[]{:S(2)}, u32[]{:S(2)}) collective-permute-start(bf16[128,1024]{1,0:T(8,128)(2,1)} %get-tuple-element.85), channel_id=1, source_target_pairs={{0,16},{1,17},{2,18},{3,19},{4,20},{5,21},{6,22},{7,23},{8,24},{9,... | collective-permute-start | bytes 786440 | tf_op jit(solution)/shard_map/ppermute | solution.py:219
  32.1 15.3 %collective-permute-start.10 = (bf16[4,32,1024]{2,1,0:T(8,128)(2,1)S(1)}, bf16[4,32,1024]{2,1,0:T(8,128)(2,1)S(1)}, u32[]{:S(2)}, u32[]{:S(2)}) collective-permute-start(bf16[4,32,1024]{2,1,0:T(8,128)(2,1)S(1)} %bitcast_dynamic-update-slice_fusion.14), channel_id=1, source_target_pairs={{0,8},{1,9},{2,10},{3,11},{4,12},{5,13},{6,14},{7,15},{8,0},{9,1},... | collective-permute-start | bytes 786440 | tf_op jit(solution)/shard_map/ppermute | solution.py:219
  34.5 18.6 %collective-permute-start.11 = (bf16[4,32,1024]{2,1,0:T(8,128)(2,1)S(1)}, bf16[4,32,1024]{2,1,0:T(8,128)(2,1)S(1)}, u32[]{:S(2)}, u32[]{:S(2)}) collective-permute-start(bf16[4,32,1024]{2,1,0:T(8,128)(2,1)S(1)} %bitcast_dynamic-update-slice_fusion.14), channel_id=1, source_target_pairs={{0,16},{1,17},{2,18},{3,19},{4,20},{5,21},{6,22},{7,23},{8,24},{9,... | collective-permute-start | bytes 786440 | tf_op jit(solution)/shard_map/ppermute | solution.py:219
  37.3 22.7 %collective-permute-start.12 = (bf16[4,32,1024]{2,1,0:T(8,128)(2,1)S(1)}, bf16[4,32,1024]{2,1,0:T(8,128)(2,1)}, u32[]{:S(2)}, u32[]{:S(2)}) collective-permute-start(bf16[4,32,1024]{2,1,0:T(8,128)(2,1)S(1)} %bitcast_dynamic-update-slice_fusion.14), channel_id=1, source_target_pairs={{0,24},{1,25},{2,26},{3,27},{4,28},{5,29},{6,30},{7,31},{8,16},{9,... | collective-permute-start | bytes 786440 | tf_op jit(solution)/shard_map/ppermute | solution.py:219
  42.3 41.2 %collective-permute-start.6 = (bf16[512,1024]{1,0:T(8,128)(2,1)S(1)}, bf16[512,1024]{1,0:T(8,128)(2,1)S(1)}, u32[]{:S(2)}, u32[]{:S(2)}) collective-permute-start(bf16[512,1024]{1,0:T(8,128)(2,1)S(1)} %get-tuple-element.58), channel_id=1, source_target_pairs={{0,1},{1,0},{2,3},{3,2},{4,5},{5,4},{6,7},{7,6},{8,9},{9,8},{10,11... | collective-permute-start | bytes 3145736 | tf_op jit(solution)/shard_map/ppermute | solution.py:219
  53.9 43.3 %all-to-all-start.2 = ((bf16[8,32,1024]{2,1,0:T(8,128)(2,1)}), bf16[8,32,1024]{2,1,0:T(8,128)(2,1)}, u32[]{:S(2)}, u32[]{:S(2)}) async-start(bf16[8,32,1024]{2,1,0:T(8,128)(2,1)} %maximum_bitcast_fusion), calls=%async_computation.2 | async-start | bytes 1048576 | tf_op jit(solution)/shard_map/all_to_all | solution.py:268
  58.0 15.6 %collective-permute-start.3 = (bf16[8,48,384]{2,1,0:T(8,128)(2,1)S(1)}, bf16[8,48,384]{2,1,0:T(8,128)(2,1)S(1)}, u32[]{:S(2)}, u32[]{:S(2)}) collective-permute-start(bf16[8,48,384]{2,1,0:T(8,128)(2,1)S(1)} %all-to-all-done), channel_id=1, source_target_pairs={{0,8},{1,9},{2,10},{3,11},{4,12},{5,13},{6,14},{7,15},{8,0},{9,1},... | collective-permute-start | bytes 884744 | tf_op jit(solution)/shard_map/ppermute | solution.py:219
  61.6 49.4 %collective-permute-start.13 = (bf16[4,4,32,1024]{3,2,1,0:T(8,128)(2,1)}, bf16[4,4,32,1024]{3,2,1,0:T(8,128)(2,1)}, u32[]{:S(2)}, u32[]{:S(2)}) collective-permute-start(bf16[4,4,32,1024]{3,2,1,0:T(8,128)(2,1)} %bitcast_dynamic-update-slice_fusion.9), channel_id=1, source_target_pairs={{0,1},{1,0},{2,3},{3,2},{4,5},{5,4},{6,7},{7,6},{8,9},{9,8},{10,11... | collective-permute-start | bytes 3145736 | tf_op jit(solution)/shard_map/ppermute | solution.py:219
  61.6 12.1 %collective-permute-start.4 = (bf16[8,48,384]{2,1,0:T(8,128)(2,1)S(1)}, bf16[8,48,384]{2,1,0:T(8,128)(2,1)S(1)}, u32[]{:S(2)}, u32[]{:S(2)}) collective-permute-start(bf16[8,48,384]{2,1,0:T(8,128)(2,1)S(1)} %all-to-all-done), channel_id=1, source_target_pairs={{0,16},{1,17},{2,18},{3,19},{4,20},{5,21},{6,22},{7,23},{8,24},{9,... | collective-permute-start | bytes 884744 | tf_op jit(solution)/shard_map/ppermute | solution.py:219
  63.1 17.2 %collective-permute-start.5 = (bf16[8,48,384]{2,1,0:T(8,128)(2,1)S(1)}, bf16[8,48,384]{2,1,0:T(8,128)(2,1)S(1)}, u32[]{:S(2)}, u32[]{:S(2)}) collective-permute-start(bf16[8,48,384]{2,1,0:T(8,128)(2,1)S(1)} %all-to-all-done), channel_id=1, source_target_pairs={{0,24},{1,25},{2,26},{3,27},{4,28},{5,29},{6,30},{7,31},{8,16},{9,... | collective-permute-start | bytes 884744 | tf_op jit(solution)/shard_map/ppermute | solution.py:219
  97.2 15.2 %all-to-all-start.1 = ((bf16[8,128,128]{2,1,0:T(8,128)(2,1)}), bf16[8,128,128]{2,1,0:T(8,128)(2,1)S(1)}, u32[]{:S(2)}, u32[]{:S(2)}) async-start(bf16[8,128,128]{2,1,0:T(8,128)(2,1)} %bitcast.20), calls=%async_computation.1 | async-start | bytes 524288 | tf_op jit(solution)/shard_map/all_to_all | solution.py:268
  102.9 28.0 %collective-permute-start.17 = (bf16[4,2,32,1024]{3,2,1,0:T(8,128)(2,1)}, bf16[4,2,32,1024]{3,2,1,0:T(8,128)(2,1)}, u32[]{:S(2)}, u32[]{:S(2)}) collective-permute-start(bf16[4,2,32,1024]{3,2,1,0:T(8,128)(2,1)} %bitcast.43), channel_id=1, source_target_pairs={{0,2},{1,3},{2,0},{3,1},{4,6},{5,7},{6,4},{7,5},{8,10},{9,11},{10,... | collective-permute-start | bytes 1572872 | tf_op jit(solution)/shard_map/ppermute | solution.py:219
  105.0 31.0 %collective-permute-start.18 = (bf16[4,2,32,1024]{3,2,1,0:T(8,128)(2,1)}, bf16[4,2,32,1024]{3,2,1,0:T(8,128)(2,1)}, u32[]{:S(2)}, u32[]{:S(2)}) collective-permute-start(bf16[4,2,32,1024]{3,2,1,0:T(8,128)(2,1)} %bitcast.43), channel_id=1, source_target_pairs={{0,4},{1,5},{2,6},{3,7},{4,0},{5,1},{6,2},{7,3},{8,12},{9,13},{10,... | collective-permute-start | bytes 1572872 | tf_op jit(solution)/shard_map/ppermute | solution.py:219
  113.9 20.3 %collective-permute-start.20 = (bf16[128,1024]{1,0:T(8,128)(2,1)S(1)}, bf16[128,1024]{1,0:T(8,128)(2,1)}, u32[]{:S(2)}, u32[]{:S(2)}) collective-permute-start(bf16[128,1024]{1,0:T(8,128)(2,1)S(1)} %add_convert_fusion.5), channel_id=1, source_target_pairs={{0,8},{1,9},{2,10},{3,11},{4,12},{5,13},{6,14},{7,15},{8,0},{9,1},... | collective-permute-start | bytes 786440 | tf_op jit(solution)/shard_map/ppermute | solution.py:219
  114.5 19.6 %collective-permute-start.21 = (bf16[128,1024]{1,0:T(8,128)(2,1)S(1)}, bf16[128,1024]{1,0:T(8,128)(2,1)S(1)}, u32[]{:S(2)}, u32[]{:S(2)}) collective-permute-start(bf16[128,1024]{1,0:T(8,128)(2,1)S(1)} %add_convert_fusion.5), channel_id=1, source_target_pairs={{0,16},{1,17},{2,18},{3,19},{4,20},{5,21},{6,22},{7,23},{8,24},{9,... | collective-permute-start | bytes 786440 | tf_op jit(solution)/shard_map/ppermute | solution.py:219
  114.9 19.3 %collective-permute-start.22 = (bf16[128,1024]{1,0:T(8,128)(2,1)S(1)}, bf16[128,1024]{1,0:T(8,128)(2,1)}, u32[]{:S(2)}, u32[]{:S(2)}) collective-permute-start(bf16[128,1024]{1,0:T(8,128)(2,1)S(1)} %add_convert_fusion.5), channel_id=1, source_target_pairs={{0,24},{1,25},{2,26},{3,27},{4,28},{5,29},{6,30},{7,31},{8,16},{9,... | collective-permute-start | bytes 786440 | tf_op jit(solution)/shard_map/ppermute | solution.py:219
  130.9 15.6 %collective-permute-start.19 = (bf16[4,2,32,1024]{3,2,1,0:T(8,128)(2,1)}, bf16[4,2,32,1024]{3,2,1,0:T(8,128)(2,1)S(1)}, u32[]{:S(2)}, u32[]{:S(2)}) collective-permute-start(bf16[4,2,32,1024]{3,2,1,0:T(8,128)(2,1)} %bitcast.43), channel_id=1, source_target_pairs={{0,6},{1,7},{2,4},{3,5},{4,2},{5,3},{6,0},{7,1},{8,14},{9,15},{10,... | collective-permute-start | bytes 1572872 | tf_op jit(solution)/shard_map/ppermute | solution.py:219
  134.2 22.6 %collective-permute-start.23 = (bf16[512,1024]{1,0:T(8,128)(2,1)}, bf16[512,1024]{1,0:T(8,128)(2,1)S(1)}, u32[]{:S(2)}, u32[]{:S(2)}) collective-permute-start(bf16[512,1024]{1,0:T(8,128)(2,1)} %pad_maximum_fusion.1.g0), channel_id=1, source_target_pairs={{0,1},{1,0},{2,3},{3,2},{4,5},{5,4},{6,7},{7,6},{8,9},{9,8},{10,11... | collective-permute-start | bytes 3145736 | tf_op jit(solution)/shard_map/ppermute | solution.py:219
  135.4 18.2 %collective-permute-start.24 = (bf16[512,1024]{1,0:T(8,128)(2,1)S(1)}, bf16[512,1024]{1,0:T(8,128)(2,1)S(1)}, u32[]{:S(2)}, u32[]{:S(2)}) collective-permute-start(bf16[512,1024]{1,0:T(8,128)(2,1)S(1)} %pad_maximum_fusion.2.m0), channel_id=1, source_target_pairs={{0,1},{1,0},{2,3},{3,2},{4,5},{5,4},{6,7},{7,6},{8,9},{9,8},{10,11... | collective-permute-start | bytes 3145736 | tf_op jit(solution)/shard_map/ppermute | solution.py:219
  169.3 32.1 %collective-permute-start.47 = (bf16[4,64,1024]{2,1,0:T(8,128)(2,1)}, bf16[4,64,1024]{2,1,0:T(8,128)(2,1)}, u32[]{:S(2)}, u32[]{:S(2)}) collective-permute-start(bf16[4,64,1024]{2,1,0:T(8,128)(2,1)} %get-tuple-element.59), channel_id=1, source_target_pairs={{0,2},{1,3},{2,0},{3,1},{4,6},{5,7},{6,4},{7,5},{8,10},{9,11},{10,... | collective-permute-start | bytes 1572872 | tf_op jit(solution)/shard_map/ppermute | solution.py:219
  179.4 38.5 %collective-permute-start.48 = (bf16[4,64,1024]{2,1,0:T(8,128)(2,1)}, bf16[4,64,1024]{2,1,0:T(8,128)(2,1)}, u32[]{:S(2)}, u32[]{:S(2)}) collective-permute-start(bf16[4,64,1024]{2,1,0:T(8,128)(2,1)} %get-tuple-element.61), channel_id=1, source_target_pairs={{0,4},{1,5},{2,6},{3,7},{4,0},{5,1},{6,2},{7,3},{8,12},{9,13},{10,... | collective-permute-start | bytes 1572872 | tf_op jit(solution)/shard_map/ppermute | solution.py:219
  179.4 38.5 %collective-permute-start.49 = (bf16[4,64,1024]{2,1,0:T(8,128)(2,1)}, bf16[4,64,1024]{2,1,0:T(8,128)(2,1)}, u32[]{:S(2)}, u32[]{:S(2)}) collective-permute-start(bf16[4,64,1024]{2,1,0:T(8,128)(2,1)} %get-tuple-element.60), channel_id=1, source_target_pairs={{0,6},{1,7},{2,4},{3,5},{4,2},{5,3},{6,0},{7,1},{8,14},{9,15},{10,... | collective-permute-start | bytes 1572872 | tf_op jit(solution)/shard_map/ppermute | solution.py:219
  184.7 50.9 %collective-permute-start.25 = (bf16[512,1024]{1,0:T(8,128)(2,1)}, bf16[512,1024]{1,0:T(8,128)(2,1)}, u32[]{:S(2)}, u32[]{:S(2)}) collective-permute-start(bf16[512,1024]{1,0:T(8,128)(2,1)} %convolution_convert_fusion.2), channel_id=1, source_target_pairs={{0,1},{1,0},{2,3},{3,2},{4,5},{5,4},{6,7},{7,6},{8,9},{9,8},{10,11... | collective-permute-start | bytes 3145736 | tf_op jit(solution)/shard_map/ppermute | solution.py:219
  220.5 13.9 %all-to-all-start.6 = ((bf16[8,32,1024]{2,1,0:T(8,128)(2,1)}), bf16[8,32,1024]{2,1,0:T(8,128)(2,1)}, u32[]{:S(2)}, u32[]{:S(2)}) async-start(bf16[8,32,1024]{2,1,0:T(8,128)(2,1)} %bitcast.219), calls=%async_computation.6 | async-start | bytes 1048576 | tf_op jit(solution)/shard_map/all_to_all | solution.py:268
  239.4 13.9 %collective-permute-start.27 = (bf16[128,1024]{1,0:T(8,128)(2,1)}, bf16[128,1024]{1,0:T(8,128)(2,1)}, u32[]{:S(2)}, u32[]{:S(2)}) collective-permute-start(bf16[128,1024]{1,0:T(8,128)(2,1)} %get-tuple-element.80), channel_id=1, source_target_pairs={{0,16},{1,17},{2,18},{3,19},{4,20},{5,21},{6,22},{7,23},{8,24},{9,... | collective-permute-start | bytes 786440 | tf_op jit(solution)/shard_map/ppermute | solution.py:219
  239.9 13.4 %collective-permute-start.28 = (bf16[128,1024]{1,0:T(8,128)(2,1)}, bf16[128,1024]{1,0:T(8,128)(2,1)}, u32[]{:S(2)}, u32[]{:S(2)}) collective-permute-start(bf16[128,1024]{1,0:T(8,128)(2,1)} %get-tuple-element.79), channel_id=1, source_target_pairs={{0,24},{1,25},{2,26},{3,27},{4,28},{5,29},{6,30},{7,31},{8,16},{9,... | collective-permute-start | bytes 786440 | tf_op jit(solution)/shard_map/ppermute | solution.py:219
  257.6 21.4 %all-to-all-start.3 = ((bf16[8,128,128]{2,1,0:T(8,128)(2,1)}), bf16[8,128,128]{2,1,0:T(8,128)(2,1)}, u32[]{:S(2)}, u32[]{:S(2)}) async-start(bf16[8,128,128]{2,1,0:T(8,128)(2,1)} %bitcast.203), calls=%async_computation.3 | async-start | bytes 524288 | tf_op jit(solution)/shard_map/all_to_all | solution.py:268
  272.2 66.0 %collective-permute-start.40 = (bf16[4,4,32,1024]{3,2,1,0:T(8,128)(2,1)}, bf16[4,4,32,1024]{3,2,1,0:T(8,128)(2,1)}, u32[]{:S(2)}, u32[]{:S(2)}) collective-permute-start(bf16[4,4,32,1024]{3,2,1,0:T(8,128)(2,1)} %dynamic-slice_bitcast_fusion), channel_id=1, source_target_pairs={{0,1},{1,0},{2,3},{3,2},{4,5},{5,4},{6,7},{7,6},{8,9},{9,8},{10,11... | collective-permute-start | bytes 3145736 | tf_op jit(solution)/shard_map/ppermute | solution.py:219
  276.0 67.6 %collective-permute-start.29 = (bf16[512,1024]{1,0:T(8,128)(2,1)}, bf16[512,1024]{1,0:T(8,128)(2,1)}, u32[]{:S(2)}, u32[]{:S(2)}) collective-permute-start(bf16[512,1024]{1,0:T(8,128)(2,1)} %convolution_convert_fusion.1), channel_id=1, source_target_pairs={{0,1},{1,0},{2,3},{3,2},{4,5},{5,4},{6,7},{7,6},{8,9},{9,8},{10,11... | collective-permute-start | bytes 3145736 | tf_op jit(solution)/shard_map/ppermute | solution.py:219
  297.7 13.2 %collective-permute-start.37 = (bf16[8,32,384]{2,1,0:T(8,128)(2,1)}, bf16[8,32,384]{2,1,0:T(8,128)(2,1)}, u32[]{:S(2)}, u32[]{:S(2)}) collective-permute-start(bf16[8,32,384]{2,1,0:T(8,128)(2,1)} %get-tuple-element.81), channel_id=1, source_target_pairs={{0,8},{1,9},{2,10},{3,11},{4,12},{5,13},{6,14},{7,15},{8,0},{9,1},... | collective-permute-start | bytes 589832 | tf_op jit(solution)/shard_map/ppermute | solution.py:219
  298.0 12.9 %collective-permute-start.38 = (bf16[8,32,384]{2,1,0:T(8,128)(2,1)}, bf16[8,32,384]{2,1,0:T(8,128)(2,1)}, u32[]{:S(2)}, u32[]{:S(2)}) collective-permute-start(bf16[8,32,384]{2,1,0:T(8,128)(2,1)} %get-tuple-element.83), channel_id=1, source_target_pairs={{0,16},{1,17},{2,18},{3,19},{4,20},{5,21},{6,22},{7,23},{8,24},{9,... | collective-permute-start | bytes 589832 | tf_op jit(solution)/shard_map/ppermute | solution.py:219
  318.2 12.3 %all-to-all-start.5 = ((bf16[8,32,384]{2,1,0:T(8,128)(2,1)}), bf16[8,32,384]{2,1,0:T(8,128)(2,1)}, u32[]{:S(2)}, u32[]{:S(2)}) async-start(bf16[8,32,384]{2,1,0:T(8,128)(2,1)} %fusion.55), calls=%async_computation.5 | async-start | bytes 393216 | tf_op jit(solution)/shard_map/all_to_all | solution.py:268
  325.9 30.4 %collective-permute-start.33 = (bf16[512,1024]{1,0:T(8,128)(2,1)}, bf16[512,1024]{1,0:T(8,128)(2,1)}, u32[]{:S(2)}, u32[]{:S(2)}) collective-permute-start(bf16[512,1024]{1,0:T(8,128)(2,1)} %get-tuple-element.33), channel_id=1, source_target_pairs={{0,1},{1,0},{2,3},{3,2},{4,5},{5,4},{6,7},{7,6},{8,9},{9,8},{10,11... | collective-permute-start | bytes 3145736 | tf_op jit(solution)/shard_map/ppermute | solution.py:219
  340.7 12.7 %collective-permute-start.42 = (bf16[4,32,1024]{2,1,0:T(8,128)(2,1)S(1)}, bf16[4,32,1024]{2,1,0:T(8,128)(2,1)S(1)}, u32[]{:S(2)}, u32[]{:S(2)}) collective-permute-start(bf16[4,32,1024]{2,1,0:T(8,128)(2,1)S(1)} %get-tuple-element.67), channel_id=1, source_target_pairs={{0,16},{1,17},{2,18},{3,19},{4,20},{5,21},{6,22},{7,23},{8,24},{9,... | collective-permute-start | bytes 786440 | tf_op jit(solution)/shard_map/ppermute | solution.py:219
  341.3 14.3 %collective-permute-start.43 = (bf16[4,32,1024]{2,1,0:T(8,128)(2,1)S(1)}, bf16[4,32,1024]{2,1,0:T(8,128)(2,1)S(1)}, u32[]{:S(2)}, u32[]{:S(2)}) collective-permute-start(bf16[4,32,1024]{2,1,0:T(8,128)(2,1)S(1)} %get-tuple-element.66), channel_id=1, source_target_pairs={{0,24},{1,25},{2,26},{3,27},{4,28},{5,29},{6,30},{7,31},{8,16},{9,... | collective-permute-start | bytes 786440 | tf_op jit(solution)/shard_map/ppermute | solution.py:219
  345.2 15.3 %collective-permute-start.30 = (bf16[128,1024]{1,0:T(8,128)(2,1)S(1)}, bf16[128,1024]{1,0:T(8,128)(2,1)S(1)}, u32[]{:S(2)}, u32[]{:S(2)}) collective-permute-start(bf16[128,1024]{1,0:T(8,128)(2,1)S(1)} %get-tuple-element.75), channel_id=1, source_target_pairs={{0,8},{1,9},{2,10},{3,11},{4,12},{5,13},{6,14},{7,15},{8,0},{9,1},... | collective-permute-start | bytes 786440 | tf_op jit(solution)/shard_map/ppermute | solution.py:219
  349.2 15.0 %collective-permute-start.31 = (bf16[128,1024]{1,0:T(8,128)(2,1)S(1)}, bf16[128,1024]{1,0:T(8,128)(2,1)S(1)}, u32[]{:S(2)}, u32[]{:S(2)}) collective-permute-start(bf16[128,1024]{1,0:T(8,128)(2,1)S(1)} %get-tuple-element.77), channel_id=1, source_target_pairs={{0,16},{1,17},{2,18},{3,19},{4,20},{5,21},{6,22},{7,23},{8,24},{9,... | collective-permute-start | bytes 786440 | tf_op jit(solution)/shard_map/ppermute | solution.py:219
  353.4 12.1 %collective-permute-start.32 = (bf16[128,1024]{1,0:T(8,128)(2,1)S(1)}, bf16[128,1024]{1,0:T(8,128)(2,1)S(1)}, u32[]{:S(2)}, u32[]{:S(2)}) collective-permute-start(bf16[128,1024]{1,0:T(8,128)(2,1)S(1)} %get-tuple-element.76), channel_id=1, source_target_pairs={{0,24},{1,25},{2,26},{3,27},{4,28},{5,29},{6,30},{7,31},{8,16},{9,... | collective-permute-start | bytes 786440 | tf_op jit(solution)/shard_map/ppermute | solution.py:219
  356.4 13.1 %collective-permute-start.45 = (bf16[32,1024]{1,0:T(8,128)(2,1)S(1)}, bf16[32,1024]{1,0:T(8,128)(2,1)S(1)}, u32[]{:S(2)}, u32[]{:S(2)}) collective-permute-start(bf16[32,1024]{1,0:T(8,128)(2,1)S(1)} %get-tuple-element.91), channel_id=1, source_target_pairs={{0,4},{1,5},{2,6},{3,7},{4,0},{5,1},{6,2},{7,3},{8,12},{9,13},{10,... | collective-permute-start | bytes 196616 | tf_op jit(solution)/shard_map/ppermute | solution.py:219
  365.5 19.2 %collective-permute-start.35 = (bf16[128,1024]{1,0:T(8,128)(2,1)S(1)}, bf16[128,1024]{1,0:T(8,128)(2,1)S(1)}, u32[]{:S(2)}, u32[]{:S(2)}) collective-permute-start(bf16[128,1024]{1,0:T(8,128)(2,1)S(1)} %get-tuple-element.74), channel_id=1, source_target_pairs={{0,4},{1,5},{2,6},{3,7},{4,0},{5,1},{6,2},{7,3},{8,12},{9,13},{10,... | collective-permute-start | bytes 786440 | tf_op jit(solution)/shard_map/ppermute | solution.py:219
  367.3 17.3 %collective-permute-start.36 = (bf16[128,1024]{1,0:T(8,128)(2,1)S(1)}, bf16[128,1024]{1,0:T(8,128)(2,1)S(1)}, u32[]{:S(2)}, u32[]{:S(2)}) collective-permute-start(bf16[128,1024]{1,0:T(8,128)(2,1)S(1)} %get-tuple-element.73), channel_id=1, source_target_pairs={{0,6},{1,7},{2,4},{3,5},{4,2},{5,3},{6,0},{7,1},{8,14},{9,15},{10,... | collective-permute-start | bytes 786440 | tf_op jit(solution)/shard_map/ppermute | solution.py:219
  (52 other events, 754.8 us)
where the time goes:
time: 390 us; the launch traced here: 386 us
  waiting for transfers between devices  131 us (34%)
  starting transfers between devices  105 us (27%)
  local copies, waits for them, and re-layouts  46.3 us (12%)
  matrix products  39.6 us (10%)
  other arithmetic  35.8 us (9%)
  Pallas kernels  26.5 us (7%)
    ppermute x50, waiting for transfers between devices, swap(): return lax.ppermute(x, ALL, pairs)  113 us
    ppermute x50, starting transfers between devices, swap(): return lax.ppermute(x, ALL, pairs)  70.6 us
    dot_general x17, matrix products, mm(): lax.dot_general(a, b, (((ca,), (cb,)), ((), ())), preferred_element_type=...  39.6 us
    all_to_all x7, starting transfers between devices, exchange(): return lax.all_to_all(x, axes, split_axis=0, concat_axis=0, tiled=True)  34.5 us
    all_to_all x7, waiting for transfers between devices, exchange(): return lax.all_to_all(x, axes, split_axis=0, concat_axis=0, tiled=True)  18 us
    dynamic_update_slice x18, local copies, waits for them, and re-layouts, place(): lax.dynamic_update_slice_in_dim(out, jnp.expand_dims(part, axis), index ^...  13.3 us
    pallas_call x1, Pallas kernels, attn_bwd(): pl.pallas_call(attn_bwd_body, grid=(n // qb,), in_specs=[pl.BlockSpec((qb...  10.5 us
    pallas_call x1, Pallas kernels, attn_fwd(): pl.pallas_call(attn_fwd_body, grid=(n // qb,), in_specs=[pl.BlockSpec((n...  9.48 us
  transfers between devices with their start and end apart: 57, of which 23 were waited for; matrix products, arithmetic and copies ran while one was open for 27% of the time, Pallas kernels for 5%

commit v1 on v0

--- a/solution.py
+++ b/solution.py
@@ -75,7 +75,7 @@
 
 
 def attn_bwd_body(
-    g_ref, log_ref, one_ref, two_ref, ok_ref, out_ref, sum_ref, all_ref, dk_acc, dv_acc
+    g_ref, log_ref, one_ref, two_ref, ok_ref, d_one, d_two, sum_ref, all_ref, dk_acc, dv_acc
 ):
     half = one_ref.shape[0]
     qb, width = g_ref.shape
@@ -114,19 +114,21 @@
     dk_acc[...] = key_sum
     dv_acc[...] = value_sum
     dq = (0.125 * jnp.concatenate(parts, axis=0).T).astype(bf16)
-    out_ref[pl.ds(step * qb, qb), :width] = dq
+    all_ref[pl.ds(step * qb, qb), :width] = dq
 
     @pl.when(step == pl.num_programs(0) - 1)
     def _():
-        out_ref[:, width : 2 * width] = dk_acc[...].astype(bf16)
-        out_ref[:, 2 * width :] = dv_acc[...].astype(bf16)
-        sum_ref[...] = jnp.sum(out_ref[...].astype(f32), axis=0, keepdims=True)
+        all_ref[:, width : 2 * width] = dk_acc[...].astype(bf16)
+        all_ref[:, 2 * width :] = dv_acc[...].astype(bf16)
+        d_one[...] = all_ref[:half]
+        d_two[...] = all_ref[half:]
+        sum_ref[...] = jnp.sum(all_ref[...].astype(f32), axis=0, keepdims=True)
 
 
 def attn_fwd(one, two, valid_col):
     n, w = valid_col.shape[0], one.shape[1] // 3
     heads = w // HD
-    qb = min(256, n)
+    qb = min(128, n)
     whole = lambda i: (0, 0)
     return pl.pallas_call(
         attn_fwd_body,
@@ -164,9 +166,14 @@
             pl.BlockSpec((n // 2, 3 * w), whole),
             pl.BlockSpec((n, 1), whole),
         ],
-        out_specs=[pl.BlockSpec((n, 3 * w), whole), pl.BlockSpec((1, 3 * w), whole)],
+        out_specs=[
+            pl.BlockSpec((n // 2, 3 * w), whole),
+            pl.BlockSpec((n // 2, 3 * w), whole),
+            pl.BlockSpec((1, 3 * w), whole),
+        ],
         out_shape=[
-            jax.ShapeDtypeStruct((n, 3 * w), bf16),
+            jax.ShapeDtypeStruct((n // 2, 3 * w), bf16),
+            jax.ShapeDtypeStruct((n // 2, 3 * w), bf16),
             jax.ShapeDtypeStruct((1, 3 * w), f32),
         ],
         scratch_shapes=[
@@ -251,9 +258,7 @@
         out = jnp.zeros(shape, block.dtype)
         for k in range(count):
             part = block if k == 0 else swap(block, **{axis_name: k})
-            out = lax.dynamic_update_slice_in_dim(
-                out, jnp.expand_dims(part, axis), index ^ k, axis
-            )
+            out = lax.dynamic_update_slice_in_dim(out, jnp.expand_dims(part, axis), index ^ k, axis)
         return out
 
     def reduce_over(x, count, axis_name, index, axis):
@@ -394,15 +399,17 @@
 
         proj_grad = mm(mid_low, attended, 0, 0).astype(bf16)
         proj_grad = reduce_over(proj_grad.reshape(F, Z, 2, R, D), 2, "kc", ci, 2)
-        proj_grad = reduce_over(proj_grad.astype(bf16), F, "kf", fi, 0)
+        proj_grad = lax.optimization_barrier(proj_grad.astype(bf16))
+        proj_grad = reduce_over(proj_grad, F, "kf", fi, 0)
         proj_grad = reduce_over(proj_grad.astype(bf16), Z, "kz", zi, 0)
         proj_grad = proj_grad.T.reshape(1, D, R)
 
-        qkv_grad, qkv_sums = attn_bwd(attended_grad, logs, qkv[0], qkv[1], valid_col)
-        qkv_halves = (qkv_grad[: N // 2], qkv_grad[N // 2 :])
+        *qkv_halves, qkv_sums = attn_bwd(attended_grad, logs, qkv[0], qkv[1], valid_col)
         in_late = mm(qkv_halves[1], w_qkv, 1, 1)
-        late_low, first = lax.optimization_barrier((in_late.astype(bf16), qkv_halves[0]))
-        in_grads = [mm(first, w_qkv, 1, 1), in_late]
+        in_late, late_low, first = lax.optimization_barrier(
+            (in_late, in_late.astype(bf16), qkv_halves[0])
+        )
+        in_grads = [lax.optimization_barrier(mm(first, w_qkv, 1, 1)), in_late]
         gain_one_grad = sum(jnp.sum(a * b, axis=0) for a, b in zip(in_grads, normed_all))
         shift_one_grad = sum(jnp.sum(a, axis=0) for a in in_grads)
         attn_in_grad = scatter_sum(in_grads[0], late_low, Z, "kz")
@@ -410,16 +417,6 @@
         images_grad = mid_grad + norm_back(attn_in_grad, normed_one, spread_one, gain_one)
 
         w_grad = sum(mm(a, g, 0, 0) for a, g in zip(attn_in, qkv_halves)).astype(bf16)
-        w_grad = reduce_over(w_grad.reshape(F, S, R, 3 * W), F, "kf", fi, 0)
-        w_grad = exchange(w_grad.astype(bf16), SEQ).astype(f32)
-        qkv_weight_grad = jnp.concatenate(
-            [
-                w_grad[..., i * W : (i + 1) * W].transpose(1, 0, 2).reshape(1, R, D)
-                for i in range(3)
-            ],
-            axis=2,
-        )
-
         my_slots = lambda part: lax.dynamic_update_slice(jnp.zeros((D,), f32), part, (si * W,))
         parts = [
             gain_one_grad,
@@ -433,8 +430,21 @@
             lax.dynamic_update_slice(jnp.zeros((FF,), f32), up_shift_grad, (pi * B,)),
         ]
         sums = jnp.concatenate([part.reshape(N_DEV, -1) for part in parts], axis=1)
-        sums = exchange(sums.reshape(N_DEV, 1, -1), ALL)
-        sums = jnp.sum(sums, axis=0)
+        sums = jnp.pad(sums.astype(bf16), ((0, 0), (0, 3 * W - sums.shape[1])))
+        sums = jnp.pad(sums.reshape(F, S, 1, 3 * W), ((0, 0), (0, 0), (0, 15), (0, 0)))
+        w_grad = jnp.concatenate([w_grad.reshape(F, S, R, 3 * W), sums], axis=2)
+        w_grad = reduce_over(w_grad, F, "kf", fi, 0)
+        w_grad = exchange(w_grad.astype(bf16), SEQ)
+        sums = jnp.sum(w_grad[:, R].astype(f32), axis=0, keepdims=True)[:, : (8 + Q) * R]
+        w_grad = w_grad[:, :R].astype(f32)
+        qkv_weight_grad = jnp.concatenate(
+            [
+                w_grad[..., i * W : (i + 1) * W].transpose(1, 0, 2).reshape(1, R, D)
+                for i in range(3)
+            ],
+            axis=2,
+        )
+
         g = [sums[:, i * R : (i + 1) * R] for i in range(8)]
         return (
             block_out[None],

time: 390 us -> 388 us (level)
  waiting for transfers between devices: 131 us -> 125 us
    all_to_all x7 -> x6, waiting for transfers between devices: 18 us -> 8.01 us  [exchange(): return lax.all_to_all(x, axes, split_axis=0, concat_axis=0, tiled=True)]
    ppermute x50, waiting for transfers between devices: 113 us -> 117 us  [swap(): return lax.ppermute(x, ALL, pairs)]
    unnamed x89 -> x92, local copies, waits for them, and re-layouts: 2.84 us -> 7.26 us
    all_to_all x7 -> x6, starting transfers between devices: 34.5 us -> 32.2 us  [exchange(): return lax.all_to_all(x, axes, split_axis=0, concat_axis=0, tiled=True)]
  transfers between devices with their start and end apart: 57 -> 56, of which waited for: 23 -> 20; matrix products, arithmetic and copies ran while one was open for 27% -> 27% of each run, Pallas kernels for 5% -> 6%
where the time goes in v1:
time: 388 us; the launch traced here: 385 us
  waiting for transfers between devices  125 us (32%)
  starting transfers between devices  104 us (27%)
  local copies, waits for them, and re-layouts  49.4 us (13%)
  matrix products  38.4 us (10%)
  other arithmetic  35.6 us (9%)
  Pallas kernels  30.4 us (8%)
    ppermute x50, waiting for transfers between devices, swap(): return lax.ppermute(x, ALL, pairs)  117 us
    ppermute x50, starting transfers between devices, swap(): return lax.ppermute(x, ALL, pairs)  71.4 us
    dot_general x17, matrix products, mm(): lax.dot_general(a, b, (((ca,), (cb,)), ((), ())), preferred_element_type=...  38.4 us
    all_to_all x6, starting transfers between devices, exchange(): return lax.all_to_all(x, axes, split_axis=0, concat_axis=0, tiled=True)  32.2 us
    dynamic_update_slice x18, local copies, waits for them, and re-layouts, place(): lax.dynamic_update_slice_in_dim(out, jnp.expand_dims(part, axis), index ^...  13.3 us
    pallas_call x1, Pallas kernels, attn_fwd(): pl.pallas_call(attn_fwd_body, grid=(n // qb,), in_specs=[pl.BlockSpec((n...  13.3 us
    pallas_call x1, Pallas kernels, attn_bwd(): pl.pallas_call(attn_bwd_body, grid=(n // qb,), in_specs=[pl.BlockSpec((qb...  10.6 us
    all_to_all x6, waiting for transfers between devices, exchange(): return lax.all_to_all(x, axes, split_axis=0, concat_axis=0, tiled=True)  8.01 us
  transfers between devices with their start and end apart: 56, of which 20 were waited for; matrix products, arithmetic and copies ran while one was open for 27% of the time, Pallas kernels for 6%

profile of v1, /device:TPU:0, one launch (start us, length us, event | category | flops | bytes accessed | tf_op | source)
XLA Modules:
  0.0 384.5 jit_solution(3705304929718826559)
XLA Ops:
  0.7 3.1 collective-permute-start.7
  3.8 2.6 collective-permute-start.8
  7.3 3.5 collective-permute-start.1
  15.5 3.6 all-to-all-start
  22.8 3.7 collective-permute-start.2
  38.3 3.6 collective-permute-done.15
  43.5 3.6 collective-permute-done.10
  47.8 5.0 %collective-permute-done.11 = bf16[4,32,1024]{2,1,0:T(8,128)(2,1)S(1)} collective-permute-done((bf16[4,32,1024]{2,1,0:T(8,128)(2,1)S(1)}, bf16[4,32,1024]{2,1,0:T(8,128)(2,1)S(1)}, u32[]{:S(2)}, u32[]{:S(2)}) %collective-permute-start.11) | collective-permute-done | bytes 262176 | tf_op jit(solution)/shard_map/ppermute | solution.py:226
  53.6 4.2 %all-to-all-start.2 = ((bf16[8,32,1024]{2,1,0:T(8,128)(2,1)}), bf16[8,32,1024]{2,1,0:T(8,128)(2,1)}, u32[]{:S(2)}, u32[]{:S(2)}) async-start(bf16[8,32,1024]{2,1,0:T(8,128)(2,1)} %maximum_bitcast_fusion), calls=%async_computation.2 | async-start | bytes 1048576 | tf_op jit(solution)/shard_map/all_to_all | solution.py:273
  63.2 10.1 %collective-permute-done.3 = bf16[8,48,384]{2,1,0:T(8,128)(2,1)S(1)} collective-permute-done((bf16[8,48,384]{2,1,0:T(8,128)(2,1)S(1)}, bf16[8,48,384]{2,1,0:T(8,128)(2,1)S(1)}, u32[]{:S(2)}, u32[]{:S(2)}) %collective-permute-start.3) | collective-permute-done | bytes 294944 | tf_op jit(solution)/shard_map/ppermute | solution.py:226
  73.5 6.5 %collective-permute-done.5 = bf16[8,48,384]{2,1,0:T(8,128)(2,1)S(1)} collective-permute-done((bf16[8,48,384]{2,1,0:T(8,128)(2,1)S(1)}, bf16[8,48,384]{2,1,0:T(8,128)(2,1)S(1)}, u32[]{:S(2)}, u32[]{:S(2)}) %collective-permute-start.5) | collective-permute-done | bytes 294944 | tf_op jit(solution)/shard_map/ppermute | solution.py:226
  86.7 13.3 %attn_fwd.1 = (bf16[1024,128]{1,0:T(8,128)(2,1)}, f32[2,1024]{1,0:T(2,128)}) custom-call(bf16[512,384]{1,0:T(8,128)(2,1)} %fusion.18.one_ref, bf16[512,384]{1,0:T(8,128)(2,1)} %fusion.19.two_ref, s32[1024,1]{1,0:T(8,128)} %copy.61.ok_ref), custom_call_target="tpu_custom_call" | custom-call | tf_op jit(solution)/shard_map/attn_fwd/pallas_call | solution.py:133
  102.0 4.4 %all-to-all-start.1 = ((bf16[8,128,128]{2,1,0:T(8,128)(2,1)}), bf16[8,128,128]{2,1,0:T(8,128)(2,1)S(1)}, u32[]{:S(2)}, u32[]{:S(2)}) async-start(bf16[8,128,128]{2,1,0:T(8,128)(2,1)} %bitcast.20), calls=%async_computation.1 | async-start | bytes 524288 | tf_op jit(solution)/shard_map/all_to_all | solution.py:273
  110.1 2.4 collective-permute-start.18
  120.7 2.6 collective-permute-start.22
  124.1 12.0 %collective-permute-done.17 = bf16[4,2,32,1024]{3,2,1,0:T(8,128)(2,1)} collective-permute-done((bf16[4,2,32,1024]{3,2,1,0:T(8,128)(2,1)}, bf16[4,2,32,1024]{3,2,1,0:T(8,128)(2,1)}, u32[]{:S(2)}, u32[]{:S(2)}) %collective-permute-start.17) | collective-permute-done | bytes 524320 | tf_op jit(solution)/shard_map/ppermute | solution.py:226
  143.1 8.5 %collective-permute-done.19 = bf16[4,2,32,1024]{3,2,1,0:T(8,128)(2,1)S(1)} collective-permute-done((bf16[4,2,32,1024]{3,2,1,0:T(8,128)(2,1)}, bf16[4,2,32,1024]{3,2,1,0:T(8,128)(2,1)S(1)}, u32[]{:S(2)}, u32[]{:S(2)}) %collective-permute-start.19) | collective-permute-done | bytes 524320 | tf_op jit(solution)/shard_map/ppermute | solution.py:226
  152.5 3.2 multiply_convert_fusion.1
  155.8 3.0 fusion.77
  158.7 3.2 multiply_convert_fusion
  162.0 3.4 fusion.76
  165.4 6.5 %ffn_grads.1 = bf16[4,4,64,1024]{3,2,1,0:T(8,128)(2,1)} custom-call(bf16[512,1024]{1,0:T(8,128)(2,1)} %copy-done.14, bf16[512,1024]{1,0:T(8,128)(2,1)} %copy-done.22, bf16[512,512]{1,0:T(8,128)(2,1)} %get-tuple-element.77.p0, bf16[512,512]{1,0:T(8,128)(2,1)} %get-tuple-element.75.p1, bf16[512,1024]{1,0:T(8,128)(2,1)} %pad_maximum_fusion.1.g0, ...), custom_call_target="tpu_custom_call" | custom-call | tf_op jit(solution)/shard_map/ffn_grads/pallas_call | solution.py:204
  171.9 2.6 dynamic-slice_bitcast_fusion.3
  174.5 10.1 %collective-permute-start.47 = (bf16[4,64,1024]{2,1,0:T(8,128)(2,1)}, bf16[4,64,1024]{2,1,0:T(8,128)(2,1)}, u32[]{:S(2)}, u32[]{:S(2)}) collective-permute-start(bf16[4,64,1024]{2,1,0:T(8,128)(2,1)} %get-tuple-element.63), channel_id=1, source_target_pairs={{0,2},{1,3},{2,0},{3,1},{4,6},{5,7},{6,4},{7,5},{8,10},{9,11},{10,... | collective-permute-start | bytes 1572872 | tf_op jit(solution)/shard_map/ppermute | solution.py:226
  184.5 2.4 collective-permute-start.49
  187.1 2.9 convolution_convert_fusion.2
  190.8 15.8 %collective-permute-done.47 = bf16[4,64,1024]{2,1,0:T(8,128)(2,1)} collective-permute-done((bf16[4,64,1024]{2,1,0:T(8,128)(2,1)}, bf16[4,64,1024]{2,1,0:T(8,128)(2,1)}, u32[]{:S(2)}, u32[]{:S(2)}) %collective-permute-start.47) | collective-permute-done | bytes 524320 | tf_op jit(solution)/shard_map/ppermute | solution.py:226
  206.6 16.4 %collective-permute-done.48 = bf16[4,64,1024]{2,1,0:T(8,128)(2,1)} collective-permute-done((bf16[4,64,1024]{2,1,0:T(8,128)(2,1)}, bf16[4,64,1024]{2,1,0:T(8,128)(2,1)}, u32[]{:S(2)}, u32[]{:S(2)}) %collective-permute-start.48) | collective-permute-done | bytes 524320 | tf_op jit(solution)/shard_map/ppermute | solution.py:226
  223.0 2.7 fusion.31
  225.7 4.2 %all-to-all-start.5 = ((bf16[8,32,1024]{2,1,0:T(8,128)(2,1)}), bf16[8,32,1024]{2,1,0:T(8,128)(2,1)}, u32[]{:S(2)}, u32[]{:S(2)}) async-start(bf16[8,32,1024]{2,1,0:T(8,128)(2,1)} %bitcast.227), calls=%async_computation.5 | async-start | bytes 1048576 | tf_op jit(solution)/shard_map/all_to_all | solution.py:273
  229.9 3.3 fusion.34
  233.3 6.3 %all-to-all-done.5 = bf16[8,32,1024]{2,1,0:T(8,128)(2,1)} async-done(((bf16[8,32,1024]{2,1,0:T(8,128)(2,1)}), bf16[8,32,1024]{2,1,0:T(8,128)(2,1)}, u32[]{:S(2)}, u32[]{:S(2)}) %all-to-all-start.5) | async-done | bytes 524320 | tf_op jit(solution)/shard_map/all_to_all | solution.py:273
  245.1 2.4 collective-permute-start.28
  253.5 5.0 %collective-permute-done.27 = bf16[128,1024]{1,0:T(8,128)(2,1)} collective-permute-done((bf16[128,1024]{1,0:T(8,128)(2,1)}, bf16[128,1024]{1,0:T(8,128)(2,1)}, u32[]{:S(2)}, u32[]{:S(2)}) %collective-permute-start.27) | collective-permute-done | bytes 262176 | tf_op jit(solution)/shard_map/ppermute | solution.py:226
  261.8 11.6 %all-to-all-start.3 = ((bf16[8,128,128]{2,1,0:T(8,128)(2,1)}), bf16[8,128,128]{2,1,0:T(8,128)(2,1)S(1)}, u32[]{:S(2)}, u32[]{:S(2)}) async-start(bf16[8,128,128]{2,1,0:T(8,128)(2,1)} %bitcast.207), calls=%async_computation.3 | async-start | bytes 524288 | tf_op jit(solution)/shard_map/all_to_all | solution.py:273
  278.4 3.0 convolution_convert_fusion.1
  284.0 10.6 %attn_bwd.1 = (bf16[512,384]{1,0:T(8,128)(2,1)}, bf16[512,384]{1,0:T(8,128)(2,1)}, f32[1,384]{1,0:T(1,128)}) custom-call(bf16[1024,128]{1,0:T(8,128)(2,1)} %bitcast.234, f32[2,1024]{1,0:T(2,128)} %get-tuple-element.32.log_ref, bf16[512,384]{1,0:T(8,128)(2,1)} %fusion.18.one_ref, bf16[512,384]{1,0:T(8,128)(2,1)} %fusion.19.two_ref, s32[1024,1]{1,0:T(8,128)} %copy.61.ok_ref), custom_call_target="tpu_custom_call" | custom-call | tf_op jit(solution)/shard_map/attn_bwd/pallas_call | solution.py:159
  294.6 2.8 fusion.84
  301.1 2.3 fusion.69
  308.2 3.3 fusion.38
  311.5 3.1 collective-permute-done.37
  314.6 4.9 %collective-permute-done.38 = bf16[8,48,384]{2,1,0:T(8,128)(2,1)S(1)} collective-permute-done((bf16[8,48,384]{2,1,0:T(8,128)(2,1)S(1)}, bf16[8,48,384]{2,1,0:T(8,128)(2,1)S(1)}, u32[]{:S(2)}, u32[]{:S(2)}) %collective-permute-start.38) | collective-permute-done | bytes 294944 | tf_op jit(solution)/shard_map/ppermute | solution.py:226
  320.4 4.3 %all-to-all-start.4 = ((bf16[8,48,384]{2,1,0:T(8,128)(2,1)}), bf16[8,48,384]{2,1,0:T(8,128)(2,1)}, u32[]{:S(2)}, u32[]{:S(2)}) async-start(bf16[8,48,384]{2,1,0:T(8,128)(2,1)} %fusion.48), calls=%async_computation.4 | async-start | bytes 589824 | tf_op jit(solution)/shard_map/all_to_all | solution.py:273
  352.1 2.4 collective-permute-start.45
  356.5 3.7 collective-permute-done.31
  361.8 2.4 collective-permute-start.35
  367.2 5.0 %collective-permute-done.34 = bf16[128,1024]{1,0:T(8,128)(2,1)S(1)} collective-permute-done((bf16[128,1024]{1,0:T(8,128)(2,1)S(1)}, bf16[128,1024]{1,0:T(8,128)(2,1)S(1)}, u32[]{:S(2)}, u32[]{:S(2)}) %collective-permute-start.34) | collective-permute-done | bytes 262176 | tf_op jit(solution)/shard_map/ppermute | solution.py:226
  372.3 10.9 %collective-permute-done.35 = bf16[128,1024]{1,0:T(8,128)(2,1)S(1)} collective-permute-done((bf16[128,1024]{1,0:T(8,128)(2,1)S(1)}, bf16[128,1024]{1,0:T(8,128)(2,1)S(1)}, u32[]{:S(2)}, u32[]{:S(2)}) %collective-permute-start.35) | collective-permute-done | bytes 262176 | tf_op jit(solution)/shard_map/ppermute | solution.py:226
  (333 shorter events, 126.6 us)
Async XLA Ops:
  0.7 22.2 %collective-permute-start.7 = (bf16[32,1024]{1,0:T(8,128)(2,1)}, bf16[32,1024]{1,0:T(8,128)(2,1)S(1)}, u32[]{:S(2)}, u32[]{:S(2)}) collective-permute-start(bf16[32,1024]{1,0:T(8,128)(2,1)} %bitcast.242), channel_id=1, source_target_pairs={{0,2},{1,3},{2,0},{3,1},{4,6},{5,7},{6,4},{7,5},{8,10},{9,11},{10,... | collective-permute-start | bytes 196616 | tf_op jit(solution)/shard_map/ppermute | solution.py:226
  3.8 22.8 %collective-permute-start.8 = (bf16[32,1024]{1,0:T(8,128)(2,1)}, bf16[32,1024]{1,0:T(8,128)(2,1)S(1)}, u32[]{:S(2)}, u32[]{:S(2)}) collective-permute-start(bf16[32,1024]{1,0:T(8,128)(2,1)} %bitcast.243), channel_id=1, source_target_pairs={{0,4},{1,5},{2,6},{3,7},{4,0},{5,1},{6,2},{7,3},{8,12},{9,13},{10,... | collective-permute-start | bytes 196616 | tf_op jit(solution)/shard_map/ppermute | solution.py:226
  6.4 21.8 %collective-permute-start.9 = (bf16[32,1024]{1,0:T(8,128)(2,1)}, bf16[32,1024]{1,0:T(8,128)(2,1)S(1)}, u32[]{:S(2)}, u32[]{:S(2)}) collective-permute-start(bf16[32,1024]{1,0:T(8,128)(2,1)} %bitcast.244), channel_id=1, source_target_pairs={{0,6},{1,7},{2,4},{3,5},{4,2},{5,3},{6,0},{7,1},{8,14},{9,15},{10,... | collective-permute-start | bytes 196616 | tf_op jit(solution)/shard_map/ppermute | solution.py:226
  6.4 25.2 %collective-permute-start = (bf16[128,1024]{1,0:T(8,128)(2,1)}, bf16[128,1024]{1,0:T(8,128)(2,1)S(1)}, u32[]{:S(2)}, u32[]{:S(2)}) collective-permute-start(bf16[128,1024]{1,0:T(8,128)(2,1)} %bitcast.215), channel_id=1, source_target_pairs={{0,2},{1,3},{2,0},{3,1},{4,6},{5,7},{6,4},{7,5},{8,10},{9,11},{10,... | collective-permute-start | bytes 786440 | tf_op jit(solution)/shard_map/ppermute | solution.py:226
  7.3 24.8 %collective-permute-start.1 = (bf16[128,1024]{1,0:T(8,128)(2,1)}, bf16[128,1024]{1,0:T(8,128)(2,1)S(1)}, u32[]{:S(2)}, u32[]{:S(2)}) collective-permute-start(bf16[128,1024]{1,0:T(8,128)(2,1)} %bitcast.216), channel_id=1, source_target_pairs={{0,4},{1,5},{2,6},{3,7},{4,0},{5,1},{6,2},{7,3},{8,12},{9,13},{10,... | collective-permute-start | bytes 786440 | tf_op jit(solution)/shard_map/ppermute | solution.py:226
  15.5 38.1 %all-to-all-start = ((bf16[8,48,384]{2,1,0:T(8,128)(2,1)}), bf16[8,48,384]{2,1,0:T(8,128)(2,1)S(1)}, u32[]{:S(2)}, u32[]{:S(2)}) async-start(bf16[8,48,384]{2,1,0:T(8,128)(2,1)} %pad_maximum_fusion.4), calls=%async_computation | async-start | bytes 589824 | tf_op jit(solution)/shard_map/all_to_all | solution.py:273
  28.2 13.8 %collective-permute-start.15 = (bf16[128,1024]{1,0:T(8,128)(2,1)S(1)}, bf16[128,1024]{1,0:T(8,128)(2,1)S(1)}, u32[]{:S(2)}, u32[]{:S(2)}) collective-permute-start(bf16[128,1024]{1,0:T(8,128)(2,1)S(1)} %get-tuple-element.88), channel_id=1, source_target_pairs={{0,16},{1,17},{2,18},{3,19},{4,20},{5,21},{6,22},{7,23},{8,24},{9,... | collective-permute-start | bytes 786440 | tf_op jit(solution)/shard_map/ppermute | solution.py:226
  32.1 15.0 %collective-permute-start.10 = (bf16[4,32,1024]{2,1,0:T(8,128)(2,1)S(1)}, bf16[4,32,1024]{2,1,0:T(8,128)(2,1)S(1)}, u32[]{:S(2)}, u32[]{:S(2)}) collective-permute-start(bf16[4,32,1024]{2,1,0:T(8,128)(2,1)S(1)} %bitcast_dynamic-update-slice_fusion.14), channel_id=1, source_target_pairs={{0,8},{1,9},{2,10},{3,11},{4,12},{5,13},{6,14},{7,15},{8,0},{9,1},... | collective-permute-start | bytes 786440 | tf_op jit(solution)/shard_map/ppermute | solution.py:226
  34.5 18.3 %collective-permute-start.11 = (bf16[4,32,1024]{2,1,0:T(8,128)(2,1)S(1)}, bf16[4,32,1024]{2,1,0:T(8,128)(2,1)S(1)}, u32[]{:S(2)}, u32[]{:S(2)}) collective-permute-start(bf16[4,32,1024]{2,1,0:T(8,128)(2,1)S(1)} %bitcast_dynamic-update-slice_fusion.14), channel_id=1, source_target_pairs={{0,16},{1,17},{2,18},{3,19},{4,20},{5,21},{6,22},{7,23},{8,24},{9,... | collective-permute-start | bytes 786440 | tf_op jit(solution)/shard_map/ppermute | solution.py:226
  36.7 23.0 %collective-permute-start.12 = (bf16[4,32,1024]{2,1,0:T(8,128)(2,1)S(1)}, bf16[4,32,1024]{2,1,0:T(8,128)(2,1)}, u32[]{:S(2)}, u32[]{:S(2)}) collective-permute-start(bf16[4,32,1024]{2,1,0:T(8,128)(2,1)S(1)} %bitcast_dynamic-update-slice_fusion.14), channel_id=1, source_target_pairs={{0,24},{1,25},{2,26},{3,27},{4,28},{5,29},{6,30},{7,31},{8,16},{9,... | collective-permute-start | bytes 786440 | tf_op jit(solution)/shard_map/ppermute | solution.py:226
  41.9 42.6 %collective-permute-start.6 = (bf16[512,1024]{1,0:T(8,128)(2,1)S(1)}, bf16[512,1024]{1,0:T(8,128)(2,1)S(1)}, u32[]{:S(2)}, u32[]{:S(2)}) collective-permute-start(bf16[512,1024]{1,0:T(8,128)(2,1)S(1)} %get-tuple-element.62), channel_id=1, source_target_pairs={{0,1},{1,0},{2,3},{3,2},{4,5},{5,4},{6,7},{7,6},{8,9},{9,8},{10,11... | collective-permute-start | bytes 3145736 | tf_op jit(solution)/shard_map/ppermute | solution.py:226
  53.6 48.4 %all-to-all-start.2 = ((bf16[8,32,1024]{2,1,0:T(8,128)(2,1)}), bf16[8,32,1024]{2,1,0:T(8,128)(2,1)}, u32[]{:S(2)}, u32[]{:S(2)}) async-start(bf16[8,32,1024]{2,1,0:T(8,128)(2,1)} %maximum_bitcast_fusion), calls=%async_computation.2 | async-start | bytes 1048576 | tf_op jit(solution)/shard_map/all_to_all | solution.py:273
  57.8 15.6 %collective-permute-start.3 = (bf16[8,48,384]{2,1,0:T(8,128)(2,1)S(1)}, bf16[8,48,384]{2,1,0:T(8,128)(2,1)S(1)}, u32[]{:S(2)}, u32[]{:S(2)}) collective-permute-start(bf16[8,48,384]{2,1,0:T(8,128)(2,1)S(1)} %all-to-all-done), channel_id=1, source_target_pairs={{0,8},{1,9},{2,10},{3,11},{4,12},{5,13},{6,14},{7,15},{8,0},{9,1},... | collective-permute-start | bytes 884744 | tf_op jit(solution)/shard_map/ppermute | solution.py:226
  61.4 54.9 %collective-permute-start.13 = (bf16[4,4,32,1024]{3,2,1,0:T(8,128)(2,1)}, bf16[4,4,32,1024]{3,2,1,0:T(8,128)(2,1)}, u32[]{:S(2)}, u32[]{:S(2)}) collective-permute-start(bf16[4,4,32,1024]{3,2,1,0:T(8,128)(2,1)} %bitcast_dynamic-update-slice_fusion.9), channel_id=1, source_target_pairs={{0,1},{1,0},{2,3},{3,2},{4,5},{5,4},{6,7},{7,6},{8,9},{9,8},{10,11... | collective-permute-start | bytes 3145736 | tf_op jit(solution)/shard_map/ppermute | solution.py:226
  62.8 17.2 %collective-permute-start.5 = (bf16[8,48,384]{2,1,0:T(8,128)(2,1)S(1)}, bf16[8,48,384]{2,1,0:T(8,128)(2,1)S(1)}, u32[]{:S(2)}, u32[]{:S(2)}) collective-permute-start(bf16[8,48,384]{2,1,0:T(8,128)(2,1)S(1)} %all-to-all-done), channel_id=1, source_target_pairs={{0,24},{1,25},{2,26},{3,27},{4,28},{5,29},{6,30},{7,31},{8,16},{9,... | collective-permute-start | bytes 884744 | tf_op jit(solution)/shard_map/ppermute | solution.py:226
  102.0 15.5 %all-to-all-start.1 = ((bf16[8,128,128]{2,1,0:T(8,128)(2,1)}), bf16[8,128,128]{2,1,0:T(8,128)(2,1)S(1)}, u32[]{:S(2)}, u32[]{:S(2)}) async-start(bf16[8,128,128]{2,1,0:T(8,128)(2,1)} %bitcast.20), calls=%async_computation.1 | async-start | bytes 524288 | tf_op jit(solution)/shard_map/all_to_all | solution.py:273
  108.0 28.0 %collective-permute-start.17 = (bf16[4,2,32,1024]{3,2,1,0:T(8,128)(2,1)}, bf16[4,2,32,1024]{3,2,1,0:T(8,128)(2,1)}, u32[]{:S(2)}, u32[]{:S(2)}) collective-permute-start(bf16[4,2,32,1024]{3,2,1,0:T(8,128)(2,1)} %bitcast.43), channel_id=1, source_target_pairs={{0,2},{1,3},{2,0},{3,1},{4,6},{5,7},{6,4},{7,5},{8,10},{9,11},{10,... | collective-permute-start | bytes 1572872 | tf_op jit(solution)/shard_map/ppermute | solution.py:226
  110.1 31.1 %collective-permute-start.18 = (bf16[4,2,32,1024]{3,2,1,0:T(8,128)(2,1)}, bf16[4,2,32,1024]{3,2,1,0:T(8,128)(2,1)}, u32[]{:S(2)}, u32[]{:S(2)}) collective-permute-start(bf16[4,2,32,1024]{3,2,1,0:T(8,128)(2,1)} %bitcast.43), channel_id=1, source_target_pairs={{0,4},{1,5},{2,6},{3,7},{4,0},{5,1},{6,2},{7,3},{8,12},{9,13},{10,... | collective-permute-start | bytes 1572872 | tf_op jit(solution)/shard_map/ppermute | solution.py:226
  119.8 19.5 %collective-permute-start.20 = (bf16[128,1024]{1,0:T(8,128)(2,1)}, bf16[128,1024]{1,0:T(8,128)(2,1)}, u32[]{:S(2)}, u32[]{:S(2)}) collective-permute-start(bf16[128,1024]{1,0:T(8,128)(2,1)} %add_convert_fusion.5), channel_id=1, source_target_pairs={{0,8},{1,9},{2,10},{3,11},{4,12},{5,13},{6,14},{7,15},{8,0},{9,1},... | collective-permute-start | bytes 786440 | tf_op jit(solution)/shard_map/ppermute | solution.py:226
  120.3 19.0 %collective-permute-start.21 = (bf16[128,1024]{1,0:T(8,128)(2,1)}, bf16[128,1024]{1,0:T(8,128)(2,1)S(1)}, u32[]{:S(2)}, u32[]{:S(2)}) collective-permute-start(bf16[128,1024]{1,0:T(8,128)(2,1)} %add_convert_fusion.5), channel_id=1, source_target_pairs={{0,16},{1,17},{2,18},{3,19},{4,20},{5,21},{6,22},{7,23},{8,24},{9,... | collective-permute-start | bytes 786440 | tf_op jit(solution)/shard_map/ppermute | solution.py:226
  120.7 18.6 %collective-permute-start.22 = (bf16[128,1024]{1,0:T(8,128)(2,1)}, bf16[128,1024]{1,0:T(8,128)(2,1)}, u32[]{:S(2)}, u32[]{:S(2)}) collective-permute-start(bf16[128,1024]{1,0:T(8,128)(2,1)} %add_convert_fusion.5), channel_id=1, source_target_pairs={{0,24},{1,25},{2,26},{3,27},{4,28},{5,29},{6,30},{7,31},{8,16},{9,... | collective-permute-start | bytes 786440 | tf_op jit(solution)/shard_map/ppermute | solution.py:226
  136.0 15.6 %collective-permute-start.19 = (bf16[4,2,32,1024]{3,2,1,0:T(8,128)(2,1)}, bf16[4,2,32,1024]{3,2,1,0:T(8,128)(2,1)S(1)}, u32[]{:S(2)}, u32[]{:S(2)}) collective-permute-start(bf16[4,2,32,1024]{3,2,1,0:T(8,128)(2,1)} %bitcast.43), channel_id=1, source_target_pairs={{0,6},{1,7},{2,4},{3,5},{4,2},{5,3},{6,0},{7,1},{8,14},{9,15},{10,... | collective-permute-start | bytes 1572872 | tf_op jit(solution)/shard_map/ppermute | solution.py:226
  139.3 22.7 %collective-permute-start.23 = (bf16[512,1024]{1,0:T(8,128)(2,1)}, bf16[512,1024]{1,0:T(8,128)(2,1)S(1)}, u32[]{:S(2)}, u32[]{:S(2)}) collective-permute-start(bf16[512,1024]{1,0:T(8,128)(2,1)} %pad_maximum_fusion.1.g0), channel_id=1, source_target_pairs={{0,1},{1,0},{2,3},{3,2},{4,5},{5,4},{6,7},{7,6},{8,9},{9,8},{10,11... | collective-permute-start | bytes 3145736 | tf_op jit(solution)/shard_map/ppermute | solution.py:226
  140.6 18.1 %collective-permute-start.24 = (bf16[512,1024]{1,0:T(8,128)(2,1)S(1)}, bf16[512,1024]{1,0:T(8,128)(2,1)S(1)}, u32[]{:S(2)}, u32[]{:S(2)}) collective-permute-start(bf16[512,1024]{1,0:T(8,128)(2,1)S(1)} %pad_maximum_fusion.2.m0), channel_id=1, source_target_pairs={{0,1},{1,0},{2,3},{3,2},{4,5},{5,4},{6,7},{7,6},{8,9},{9,8},{10,11... | collective-permute-start | bytes 3145736 | tf_op jit(solution)/shard_map/ppermute | solution.py:226
  174.5 32.1 %collective-permute-start.47 = (bf16[4,64,1024]{2,1,0:T(8,128)(2,1)}, bf16[4,64,1024]{2,1,0:T(8,128)(2,1)}, u32[]{:S(2)}, u32[]{:S(2)}) collective-permute-start(bf16[4,64,1024]{2,1,0:T(8,128)(2,1)} %get-tuple-element.63), channel_id=1, source_target_pairs={{0,2},{1,3},{2,0},{3,1},{4,6},{5,7},{6,4},{7,5},{8,10},{9,11},{10,... | collective-permute-start | bytes 1572872 | tf_op jit(solution)/shard_map/ppermute | solution.py:226
  184.5 38.5 %collective-permute-start.48 = (bf16[4,64,1024]{2,1,0:T(8,128)(2,1)}, bf16[4,64,1024]{2,1,0:T(8,128)(2,1)}, u32[]{:S(2)}, u32[]{:S(2)}) collective-permute-start(bf16[4,64,1024]{2,1,0:T(8,128)(2,1)} %get-tuple-element.65), channel_id=1, source_target_pairs={{0,4},{1,5},{2,6},{3,7},{4,0},{5,1},{6,2},{7,3},{8,12},{9,13},{10,... | collective-permute-start | bytes 1572872 | tf_op jit(solution)/shard_map/ppermute | solution.py:226
  184.5 38.5 %collective-permute-start.49 = (bf16[4,64,1024]{2,1,0:T(8,128)(2,1)}, bf16[4,64,1024]{2,1,0:T(8,128)(2,1)}, u32[]{:S(2)}, u32[]{:S(2)}) collective-permute-start(bf16[4,64,1024]{2,1,0:T(8,128)(2,1)} %get-tuple-element.64), channel_id=1, source_target_pairs={{0,6},{1,7},{2,4},{3,5},{4,2},{5,3},{6,0},{7,1},{8,14},{9,15},{10,... | collective-permute-start | bytes 1572872 | tf_op jit(solution)/shard_map/ppermute | solution.py:226
  190.1 50.7 %collective-permute-start.25 = (bf16[512,1024]{1,0:T(8,128)(2,1)}, bf16[512,1024]{1,0:T(8,128)(2,1)}, u32[]{:S(2)}, u32[]{:S(2)}) collective-permute-start(bf16[512,1024]{1,0:T(8,128)(2,1)} %convolution_convert_fusion.2), channel_id=1, source_target_pairs={{0,1},{1,0},{2,3},{3,2},{4,5},{5,4},{6,7},{7,6},{8,9},{9,8},{10,11... | collective-permute-start | bytes 3145736 | tf_op jit(solution)/shard_map/ppermute | solution.py:226
  225.7 13.9 %all-to-all-start.5 = ((bf16[8,32,1024]{2,1,0:T(8,128)(2,1)}), bf16[8,32,1024]{2,1,0:T(8,128)(2,1)}, u32[]{:S(2)}, u32[]{:S(2)}) async-start(bf16[8,32,1024]{2,1,0:T(8,128)(2,1)} %bitcast.227), calls=%async_computation.5 | async-start | bytes 1048576 | tf_op jit(solution)/shard_map/all_to_all | solution.py:273
  244.5 13.9 %collective-permute-start.27 = (bf16[128,1024]{1,0:T(8,128)(2,1)}, bf16[128,1024]{1,0:T(8,128)(2,1)}, u32[]{:S(2)}, u32[]{:S(2)}) collective-permute-start(bf16[128,1024]{1,0:T(8,128)(2,1)} %get-tuple-element.86), channel_id=1, source_target_pairs={{0,16},{1,17},{2,18},{3,19},{4,20},{5,21},{6,22},{7,23},{8,24},{9,... | collective-permute-start | bytes 786440 | tf_op jit(solution)/shard_map/ppermute | solution.py:226
  245.1 13.4 %collective-permute-start.28 = (bf16[128,1024]{1,0:T(8,128)(2,1)}, bf16[128,1024]{1,0:T(8,128)(2,1)}, u32[]{:S(2)}, u32[]{:S(2)}) collective-permute-start(bf16[128,1024]{1,0:T(8,128)(2,1)} %get-tuple-element.85), channel_id=1, source_target_pairs={{0,24},{1,25},{2,26},{3,27},{4,28},{5,29},{6,30},{7,31},{8,16},{9,... | collective-permute-start | bytes 786440 | tf_op jit(solution)/shard_map/ppermute | solution.py:226
  261.8 21.3 %all-to-all-start.3 = ((bf16[8,128,128]{2,1,0:T(8,128)(2,1)}), bf16[8,128,128]{2,1,0:T(8,128)(2,1)S(1)}, u32[]{:S(2)}, u32[]{:S(2)}) async-start(bf16[8,128,128]{2,1,0:T(8,128)(2,1)} %bitcast.207), calls=%async_computation.3 | async-start | bytes 524288 | tf_op jit(solution)/shard_map/all_to_all | solution.py:273
  277.6 47.1 %collective-permute-start.40 = (bf16[4,4,32,1024]{3,2,1,0:T(8,128)(2,1)}, bf16[4,4,32,1024]{3,2,1,0:T(8,128)(2,1)}, u32[]{:S(2)}, u32[]{:S(2)}) collective-permute-start(bf16[4,4,32,1024]{3,2,1,0:T(8,128)(2,1)} %dynamic-slice_bitcast_fusion), channel_id=1, source_target_pairs={{0,1},{1,0},{2,3},{3,2},{4,5},{5,4},{6,7},{7,6},{8,9},{9,8},{10,11... | collective-permute-start | bytes 3145736 | tf_op jit(solution)/shard_map/ppermute | solution.py:226
  281.4 50.9 %collective-permute-start.29 = (bf16[512,1024]{1,0:T(8,128)(2,1)}, bf16[512,1024]{1,0:T(8,128)(2,1)}, u32[]{:S(2)}, u32[]{:S(2)}) collective-permute-start(bf16[512,1024]{1,0:T(8,128)(2,1)} %convolution_convert_fusion.1), channel_id=1, source_target_pairs={{0,1},{1,0},{2,3},{3,2},{4,5},{5,4},{6,7},{7,6},{8,9},{9,8},{10,11... | collective-permute-start | bytes 3145736 | tf_op jit(solution)/shard_map/ppermute | solution.py:226
  305.0 14.5 %collective-permute-start.38 = (bf16[8,48,384]{2,1,0:T(8,128)(2,1)S(1)}, bf16[8,48,384]{2,1,0:T(8,128)(2,1)S(1)}, u32[]{:S(2)}, u32[]{:S(2)}) collective-permute-start(bf16[8,48,384]{2,1,0:T(8,128)(2,1)S(1)} %get-tuple-element.68), channel_id=1, source_target_pairs={{0,16},{1,17},{2,18},{3,19},{4,20},{5,21},{6,22},{7,23},{8,24},{9,... | collective-permute-start | bytes 884744 | tf_op jit(solution)/shard_map/ppermute | solution.py:226
  306.4 13.0 %collective-permute-start.39 = (bf16[8,48,384]{2,1,0:T(8,128)(2,1)S(1)}, bf16[8,48,384]{2,1,0:T(8,128)(2,1)S(1)}, u32[]{:S(2)}, u32[]{:S(2)}) collective-permute-start(bf16[8,48,384]{2,1,0:T(8,128)(2,1)S(1)} %get-tuple-element.67), channel_id=1, source_target_pairs={{0,24},{1,25},{2,26},{3,27},{4,28},{5,29},{6,30},{7,31},{8,16},{9,... | collective-permute-start | bytes 884744 | tf_op jit(solution)/shard_map/ppermute | solution.py:226
  314.6 37.5 %collective-permute-start.33 = (bf16[512,1024]{1,0:T(8,128)(2,1)}, bf16[512,1024]{1,0:T(8,128)(2,1)}, u32[]{:S(2)}, u32[]{:S(2)}) collective-permute-start(bf16[512,1024]{1,0:T(8,128)(2,1)} %get-tuple-element.36), channel_id=1, source_target_pairs={{0,1},{1,0},{2,3},{3,2},{4,5},{5,4},{6,7},{7,6},{8,9},{9,8},{10,11... | collective-permute-start | bytes 3145736 | tf_op jit(solution)/shard_map/ppermute | solution.py:226
  320.4 17.1 %all-to-all-start.4 = ((bf16[8,48,384]{2,1,0:T(8,128)(2,1)}), bf16[8,48,384]{2,1,0:T(8,128)(2,1)}, u32[]{:S(2)}, u32[]{:S(2)}) async-start(bf16[8,48,384]{2,1,0:T(8,128)(2,1)} %fusion.48), calls=%async_computation.4 | async-start | bytes 589824 | tf_op jit(solution)/shard_map/all_to_all | solution.py:273
  328.7 18.2 %collective-permute-start.41 = (bf16[4,32,1024]{2,1,0:T(8,128)(2,1)}, bf16[4,32,1024]{2,1,0:T(8,128)(2,1)}, u32[]{:S(2)}, u32[]{:S(2)}) collective-permute-start(bf16[4,32,1024]{2,1,0:T(8,128)(2,1)} %get-tuple-element.71), channel_id=1, source_target_pairs={{0,8},{1,9},{2,10},{3,11},{4,12},{5,13},{6,14},{7,15},{8,0},{9,1},... | collective-permute-start | bytes 786440 | tf_op jit(solution)/shard_map/ppermute | solution.py:226
  330.4 17.0 %collective-permute-start.42 = (bf16[4,32,1024]{2,1,0:T(8,128)(2,1)}, bf16[4,32,1024]{2,1,0:T(8,128)(2,1)}, u32[]{:S(2)}, u32[]{:S(2)}) collective-permute-start(bf16[4,32,1024]{2,1,0:T(8,128)(2,1)} %get-tuple-element.73), channel_id=1, source_target_pairs={{0,16},{1,17},{2,18},{3,19},{4,20},{5,21},{6,22},{7,23},{8,24},{9,... | collective-permute-start | bytes 786440 | tf_op jit(solution)/shard_map/ppermute | solution.py:226
  330.8 18.1 %collective-permute-start.43 = (bf16[4,32,1024]{2,1,0:T(8,128)(2,1)}, bf16[4,32,1024]{2,1,0:T(8,128)(2,1)}, u32[]{:S(2)}, u32[]{:S(2)}) collective-permute-start(bf16[4,32,1024]{2,1,0:T(8,128)(2,1)} %get-tuple-element.72), channel_id=1, source_target_pairs={{0,24},{1,25},{2,26},{3,27},{4,28},{5,29},{6,30},{7,31},{8,16},{9,... | collective-permute-start | bytes 786440 | tf_op jit(solution)/shard_map/ppermute | solution.py:226
  335.8 20.3 %collective-permute-start.30 = (bf16[128,1024]{1,0:T(8,128)(2,1)}, bf16[128,1024]{1,0:T(8,128)(2,1)}, u32[]{:S(2)}, u32[]{:S(2)}) collective-permute-start(bf16[128,1024]{1,0:T(8,128)(2,1)} %get-tuple-element.81), channel_id=1, source_target_pairs={{0,8},{1,9},{2,10},{3,11},{4,12},{5,13},{6,14},{7,15},{8,0},{9,1},... | collective-permute-start | bytes 786440 | tf_op jit(solution)/shard_map/ppermute | solution.py:226
  347.0 13.2 %collective-permute-start.31 = (bf16[128,1024]{1,0:T(8,128)(2,1)}, bf16[128,1024]{1,0:T(8,128)(2,1)S(1)}, u32[]{:S(2)}, u32[]{:S(2)}) collective-permute-start(bf16[128,1024]{1,0:T(8,128)(2,1)} %get-tuple-element.83), channel_id=1, source_target_pairs={{0,16},{1,17},{2,18},{3,19},{4,20},{5,21},{6,22},{7,23},{8,24},{9,... | collective-permute-start | bytes 786440 | tf_op jit(solution)/shard_map/ppermute | solution.py:226
  347.4 14.4 %collective-permute-start.32 = (bf16[128,1024]{1,0:T(8,128)(2,1)}, bf16[128,1024]{1,0:T(8,128)(2,1)S(1)}, u32[]{:S(2)}, u32[]{:S(2)}) collective-permute-start(bf16[128,1024]{1,0:T(8,128)(2,1)} %get-tuple-element.82), channel_id=1, source_target_pairs={{0,24},{1,25},{2,26},{3,27},{4,28},{5,29},{6,30},{7,31},{8,16},{9,... | collective-permute-start | bytes 786440 | tf_op jit(solution)/shard_map/ppermute | solution.py:226
  350.3 13.9 %collective-permute-start.44 = (bf16[32,1024]{1,0:T(8,128)(2,1)S(1)}, bf16[32,1024]{1,0:T(8,128)(2,1)S(1)}, u32[]{:S(2)}, u32[]{:S(2)}) collective-permute-start(bf16[32,1024]{1,0:T(8,128)(2,1)S(1)} %get-tuple-element.92), channel_id=1, source_target_pairs={{0,2},{1,3},{2,0},{3,1},{4,6},{5,7},{6,4},{7,5},{8,10},{9,11},{10,... | collective-permute-start | bytes 196616 | tf_op jit(solution)/shard_map/ppermute | solution.py:226
  352.1 14.4 %collective-permute-start.45 = (bf16[32,1024]{1,0:T(8,128)(2,1)S(1)}, bf16[32,1024]{1,0:T(8,128)(2,1)S(1)}, u32[]{:S(2)}, u32[]{:S(2)}) collective-permute-start(bf16[32,1024]{1,0:T(8,128)(2,1)S(1)} %get-tuple-element.94), channel_id=1, source_target_pairs={{0,4},{1,5},{2,6},{3,7},{4,0},{5,1},{6,2},{7,3},{8,12},{9,13},{10,... | collective-permute-start | bytes 196616 | tf_op jit(solution)/shard_map/ppermute | solution.py:226
  361.8 21.3 %collective-permute-start.35 = (bf16[128,1024]{1,0:T(8,128)(2,1)S(1)}, bf16[128,1024]{1,0:T(8,128)(2,1)S(1)}, u32[]{:S(2)}, u32[]{:S(2)}) collective-permute-start(bf16[128,1024]{1,0:T(8,128)(2,1)S(1)} %get-tuple-element.80), channel_id=1, source_target_pairs={{0,4},{1,5},{2,6},{3,7},{4,0},{5,1},{6,2},{7,3},{8,12},{9,13},{10,... | collective-permute-start | bytes 786440 | tf_op jit(solution)/shard_map/ppermute | solution.py:226
  364.2 19.0 %collective-permute-start.36 = (bf16[128,1024]{1,0:T(8,128)(2,1)S(1)}, bf16[128,1024]{1,0:T(8,128)(2,1)S(1)}, u32[]{:S(2)}, u32[]{:S(2)}) collective-permute-start(bf16[128,1024]{1,0:T(8,128)(2,1)S(1)} %get-tuple-element.79), channel_id=1, source_target_pairs={{0,6},{1,7},{2,4},{3,5},{4,2},{5,3},{6,0},{7,1},{8,14},{9,15},{10,... | collective-permute-start | bytes 786440 | tf_op jit(solution)/shard_map/ppermute | solution.py:226
  (52 other events, 500.4 us)
